TPU v7x, 512 devices: a whole 4x4x16 slice. The times are simulated.
512 devices in a mesh: depth: 32 (over z_hi, y, core), strip: 4 (over z_lo), freq: 4 (over x).
Axes of the slice: x: 4, y: 4, z: 16 (z_hi: 4, z_lo: 4; z = z_hi * 4 + z_lo), core: 2. Of those that a mesh axis runs over, the one named last changes fastest.
Arguments:
- down_state: float32 [64, 2, 8, 32, 1024], P('depth', None, 'freq', 'strip'), may hold values from -6 to 6
- up_state: float32 [64, 2, 8, 32, 1024], P('depth', None, 'freq', 'strip'), may hold values from -6 to 6
- reflect: float32 [64, 32, 1024], P('depth', 'strip'), may hold values from -3 to 3
- layer_mask: int32 [64, 32, 1024], P('depth', 'strip'), may hold values 0 or 1
- classes: int32 [64, 32, 1024], P('depth', 'strip'), may hold values from 0 to 63
- coeffs: float32 [64, 2, 8, 8], P(None, None, 'freq'), may hold values from -1.2 to 1.2
Outputs:
- down_out: float32 [64, 2, 8, 32, 1024], P('depth', None, 'freq', 'strip')
- up_out: float32 [64, 2, 8, 32, 1024], P('depth', None, 'freq', 'strip')
- image: float32 [64, 32, 1024], P('depth', 'strip', 'freq')
All inputs are finite; a program needn't handle non-finite values. No bound on the sum of `layer_mask` on one device may be relied on, other than what follows from the above.
Results may differ from a plain program's by a relative error of at most 0.0003.
Values sent between devices are 32-bit elements; how exact they have to be, the bound alone decides.
No kernel may reach another device: no remote copies, remote signals or barrier semaphores. Data moves between devices by JAX's collectives and lax.ppermute only.
A program may use at most 64 MiB of HBM per device.

v0:
```python
import jax
import jax.numpy as jnp
from jax import lax
from jax.sharding import PartitionSpec as P

TICKS = 2
TERMS = 8
CLASSES = 64


def extended(cells, sides, width):
    for axis, dim in sides:
        count = lax.axis_size(axis)
        ends = count - 1
        head = lax.slice_in_dim(cells, 0, width, axis=dim)
        tail = lax.slice_in_dim(cells, cells.shape[dim] - width, cells.shape[dim], axis=dim)
        cells = jnp.concatenate(
            [
                lax.ppermute(tail, axis, [(i, (i + 1) % count) for i in range(ends)]),
                cells,
                lax.ppermute(head, axis, [((i + 1) % count, i) for i in range(ends)]),
            ],
            axis=dim,
        )
    return cells


def passed_along(block, axis, distance):
    devices = range(lax.axis_size(axis))
    route = [(i - distance, i) for i in devices if i - distance in devices]
    return lax.ppermute(block, axis, route)


def lateral(widened):
    padded = jnp.pad(widened, ((0, 0), (0, 0), (0, 0), (1, 1)))
    return (
        widened[:, :, 2:] + widened[:, :, :-2] + (padded[:, :, 1:-1, 2:] + padded[:, :, 1:-1, :-2])
    ) * 0.25


def chebyshev_terms(wavefield):
    terms = [wavefield]
    for order in range(1, TERMS):
        spread = lateral(extended(terms[-1], (("strip", 2),), 1))
        if order == 1:
            terms.append(spread)
        else:
            terms.append(2.0 * spread - terms[-2])
    return terms


def combine_terms(terms, table):
    real_sum = table[0, :, 0] * terms[0][0] - table[1, :, 0] * terms[0][1]
    imag_sum = table[0, :, 0] * terms[0][1] + table[1, :, 0] * terms[0][0]
    for order in range(1, TERMS):
        real_sum = real_sum + (
            table[0, :, order] * terms[order][0] - table[1, :, order] * terms[order][1]
        )
        imag_sum = imag_sum + (
            table[0, :, order] * terms[order][1] + table[1, :, order] * terms[order][0]
        )
    return jnp.stack([real_sum, imag_sum])


def filter_fields(fields, tables):
    stacked = fields[0]
    terms = chebyshev_terms(stacked)
    picked = [term for term in terms]
    results = [combine_terms(picked, tables[0])]
    return results


def level_table(cell_classes, coeffs):
    width_rows, columns = cell_classes.shape
    freqs_here = coeffs.shape[2]
    onehot = (
        jnp.arange(CLASSES, dtype=jnp.int32)[:, None]
        == cell_classes.reshape(1, width_rows * columns)
    ).astype(jnp.float32)
    flat = coeffs.reshape(CLASSES, 2 * freqs_here * TERMS)
    table = jnp.dot(
        flat.T, onehot, precision=lax.Precision.HIGHEST, preferred_element_type=jnp.float32
    )
    return table.reshape(2, freqs_here, TERMS, width_rows, columns)


def local(down_state, up_state, reflect, layer_mask, classes, coeffs):
    levels_here = down_state.shape[0]
    coupling = reflect * layer_mask.astype(jnp.float32)
    tables = [level_table(classes[level], coeffs) for level in range(levels_here)]
    down = down_state
    upward = up_state
    for tick in range(TICKS):
        entry_down = passed_along(down[levels_here - 1], "depth", 1)
        entry_up = passed_along(upward[0], "depth", -1)
        running = entry_down
        new_down = []
        for level in range(levels_here):
            running = filter_fields(
                [running + coupling[level][None, None] * upward[level]], [tables[level]]
            )[0]
            new_down.append(running)
        running = entry_up
        new_up = [None] * levels_here
        for level in range(levels_here - 1, -1, -1):
            running = filter_fields(
                [running + coupling[level][None, None] * down[level]], [tables[level]]
            )[0]
            new_up[level] = running
        down = jnp.stack(new_down)
        upward = jnp.stack(new_up)
    correlation = jnp.sum(down[:, 0] * upward[:, 0] + down[:, 1] * upward[:, 1], axis=1)
    illumination = jnp.sum(down[:, 0] * down[:, 0] + down[:, 1] * down[:, 1], axis=1)
    totals = lax.psum((correlation, illumination), "freq")
    share = correlation.shape[2] // lax.axis_size("freq")
    offset = lax.axis_index("freq") * share
    corr_part = lax.dynamic_slice_in_dim(totals[0], offset, share, 2)
    illum_part = lax.dynamic_slice_in_dim(totals[1], offset, share, 2)
    image = corr_part / (1.0 + illum_part)
    return (down, upward, image)


def solution(mesh):
    placed = (
        P("depth", None, "freq", "strip", None),
        P("depth", None, "freq", "strip", None),
        P("depth", "strip", None),
        P("depth", "strip", None),
        P("depth", "strip", None),
        P(None, None, "freq", None),
    )
    return jax.shard_map(
        local,
        mesh=mesh,
        in_specs=placed,
        out_specs=(
            P("depth", None, "freq", "strip", None),
            P("depth", None, "freq", "strip", None),
            P("depth", "strip", "freq"),
        ),
        check_vma=False,
    )
```

profile of v0, /device:TPU:25, one launch (start us, length us, event | category | flops | bytes accessed | tf_op | source)
XLA Modules:
  0.0 505.3 jit_solution(5314863248542149515)
XLA Ops:
  11.8 8.9 %collective-permute-done.30 = f32[2,2,8,1024]{3,2,1,0:T(8,128)S(1)} collective-permute-done((f32[2,2,8,1024]{3,2,1,0:T(8,128)S(1)}, f32[2,2,8,1024]{3,2,1,0:T(8,128)S(1)}, u32[]{:S(2)}, u32[]{:S(2)}) %collective-permute-start.30) | collective-permute-done | bytes 131104 | tf_op jit(solution)/shard_map/ppermute | solution.py:31
  22.9 4.4 collective-permute-start.32
  37.7 4.3 collective-permute-start.36
  44.5 4.3 collective-permute-start.38
  64.9 4.3 collective-permute-start.44
  123.6 4.8 collective-permute-start.54
  148.7 4.5 collective-permute-start.16
  155.8 4.3 collective-permute-start.18
  173.6 4.3 collective-permute-start.22
  180.4 4.3 collective-permute-start.24
  193.9 4.3 collective-permute-start.28
  198.2 24.1 %collective-permute-start.87 = (f32[2,2,8,1024]{3,2,1,0:T(8,128)S(1)}, f32[2,2,8,1024]{3,2,1,0:T(8,128)S(1)}, u32[]{:S(2)}, u32[]{:S(2)}) collective-permute-start(f32[2,2,8,1024]{3,2,1,0:T(8,128)S(1)} %pad_maximum_fusion.117), channel_id=1, source_target_pairs={{16,0},{32,16},{48,32},{64,48},{80,64},{96,80},{112,96},{128,112},... | collective-permute-start | bytes 393224 | tf_op jit(solution)/shard_map/ppermute | solution.py:31
  227.3 7.1 %collective-permute-start.89 = (f32[2,2,1,1024]{3,2,1,0:T(1,128)S(1)}, f32[2,2,1,1024]{3,2,1,0:T(1,128)S(1)}, u32[]{:S(2)}, u32[]{:S(2)}) collective-permute-start(f32[2,2,1,1024]{3,2,1,0:T(1,128)S(1)} %get-tuple-element.67), channel_id=1, source_target_pairs={{0,4},{4,8},{8,12},{1,5},{5,9},{9,13},{2,6},{6,10},{10,14},{3,7},{... | collective-permute-start | bytes 49160 | tf_op jit(solution)/shard_map/ppermute | solution.py:19
  236.9 4.3 collective-permute-start.91
  250.5 4.3 collective-permute-start.95
  257.3 4.3 collective-permute-start.97
  264.1 4.3 collective-permute-start.99
  271.0 4.3 collective-permute-start.101
  275.2 9.0 %collective-permute-start.29 = (f32[2,2,8,1024]{3,2,1,0:T(8,128)}, f32[2,2,8,1024]{3,2,1,0:T(8,128)S(1)}, u32[]{:S(2)}, u32[]{:S(2)}) collective-permute-start(f32[2,2,8,1024]{3,2,1,0:T(8,128)} %get-tuple-element.70), channel_id=1, source_target_pairs={{0,16},{16,32},{32,48},{48,64},{64,80},{80,96},{96,112},{112,128},... | collective-permute-start | bytes 393224 | tf_op jit(solution)/shard_map/ppermute | solution.py:31
  287.6 5.1 %collective-permute-start.60 = (f32[2,2,1,1024]{3,2,1,0:T(1,128)S(1)}, f32[2,2,1,1024]{3,2,1,0:T(1,128)S(1)}, u32[]{:S(2)}, u32[]{:S(2)}) collective-permute-start(f32[2,2,1,1024]{3,2,1,0:T(1,128)S(1)} %get-tuple-element.99), channel_id=1, source_target_pairs={{0,4},{4,8},{8,12},{1,5},{5,9},{9,13},{2,6},{6,10},{10,14},{3,7},{... | collective-permute-start | bytes 49160 | tf_op jit(solution)/shard_map/ppermute | solution.py:19
  294.1 5.1 %collective-permute-start.103 = (f32[2,2,1,1024]{3,2,1,0:T(1,128)S(1)}, f32[2,2,1,1024]{3,2,1,0:T(1,128)S(1)}, u32[]{:S(2)}, u32[]{:S(2)}) collective-permute-start(f32[2,2,1,1024]{3,2,1,0:T(1,128)S(1)} %get-tuple-element.51), channel_id=1, source_target_pairs={{0,4},{4,8},{8,12},{1,5},{5,9},{9,13},{2,6},{6,10},{10,14},{3,7},{... | collective-permute-start | bytes 49160 | tf_op jit(solution)/shard_map/ppermute | solution.py:19
  371.8 4.3 collective-permute-start.76
  389.6 4.3 collective-permute-start.80
  418.2 78.9 %all-reduce.59.cloned.1.call-done = (f32[2,8,1024]{2,1,0:T(8,128)}, f32[2,8,1024]{2,1,0:T(8,128)}) async-done(((f32[2,8,1024]{2,1,0:T(8,128)}, f32[2,8,1024]{2,1,0:T(8,128)}), (f32[2,8,1024]{2,1,0:T(8,128)}, f32[2,8,1024]{2,1,0:T(8,128)})) %all-reduce.59.cloned.1.call-update) | async-done | bytes 131088 | tf_op jit(solution)/shard_map/psum | solution.py:114
  (426 shorter events, 277.1 us)
Async XLA Ops:
  7.2 489.9 %all-reduce.59.cloned.1.call-start = ((), (), s32[]{:S(2)}) async-start(), calls=%async_computation | async-start | bytes 262144 | tf_op jit(solution)/shard_map/psum | solution.py:114
  8.2 12.5 %collective-permute-start.30 = (f32[2,2,8,1024]{3,2,1,0:T(8,128)S(1)}, f32[2,2,8,1024]{3,2,1,0:T(8,128)S(1)}, u32[]{:S(2)}, u32[]{:S(2)}) collective-permute-start(f32[2,2,8,1024]{3,2,1,0:T(8,128)S(1)} %slice_bitcast_fusion), channel_id=1, source_target_pairs={{16,0},{32,16},{48,32},{64,48},{80,64},{96,80},{112,96},{128,112},... | collective-permute-start | bytes 393224 | tf_op jit(solution)/shard_map/ppermute | solution.py:31
  27.3 43.9 %collective-permute-start = (f32[2,2,8,1024]{3,2,1,0:T(8,128)S(1)}, f32[2,2,8,1024]{3,2,1,0:T(8,128)S(1)}, u32[]{:S(2)}, u32[]{:S(2)}) collective-permute-start(f32[2,2,8,1024]{3,2,1,0:T(8,128)S(1)} %slice_bitcast_fusion.1), channel_id=1, source_target_pairs={{0,16},{16,32},{32,48},{48,64},{64,80},{80,96},{96,112},{112,128},... | collective-permute-start | bytes 393224 | tf_op jit(solution)/shard_map/ppermute | solution.py:31
  77.3 11.1 %collective-permute-start.45 = (f32[2,2,1,1024]{3,2,1,0:T(1,128)S(1)}, f32[2,2,1,1024]{3,2,1,0:T(1,128)S(1)}, u32[]{:S(2)}, u32[]{:S(2)}) collective-permute-start(f32[2,2,1,1024]{3,2,1,0:T(1,128)S(1)} %get-tuple-element.114), channel_id=1, source_target_pairs={{4,0},{8,4},{12,8},{5,1},{9,5},{13,9},{6,2},{10,6},{14,10},{7,3},{... | collective-permute-start | bytes 49160 | tf_op jit(solution)/shard_map/ppermute | solution.py:21
  88.8 11.0 %collective-permute-start.47 = (f32[2,2,1,1024]{3,2,1,0:T(1,128)S(1)}, f32[2,2,1,1024]{3,2,1,0:T(1,128)S(1)}, u32[]{:S(2)}, u32[]{:S(2)}) collective-permute-start(f32[2,2,1,1024]{3,2,1,0:T(1,128)S(1)} %get-tuple-element.112), channel_id=1, source_target_pairs={{4,0},{8,4},{12,8},{5,1},{9,5},{13,9},{6,2},{10,6},{14,10},{7,3},{... | collective-permute-start | bytes 49160 | tf_op jit(solution)/shard_map/ppermute | solution.py:21
  94.5 11.0 %collective-permute-start.5 = (f32[2,2,1,1024]{3,2,1,0:T(1,128)S(1)}, f32[2,2,1,1024]{3,2,1,0:T(1,128)S(1)}, u32[]{:S(2)}, u32[]{:S(2)}) collective-permute-start(f32[2,2,1,1024]{3,2,1,0:T(1,128)S(1)} %get-tuple-element.152), channel_id=1, source_target_pairs={{4,0},{8,4},{12,8},{5,1},{9,5},{13,9},{6,2},{10,6},{14,10},{7,3},{... | collective-permute-start | bytes 49160 | tf_op jit(solution)/shard_map/ppermute | solution.py:21
  117.2 11.2 %collective-permute-start.10 = (f32[2,2,1,1024]{3,2,1,0:T(1,128)S(1)}, f32[2,2,1,1024]{3,2,1,0:T(1,128)S(1)}, u32[]{:S(2)}, u32[]{:S(2)}) collective-permute-start(f32[2,2,1,1024]{3,2,1,0:T(1,128)S(1)} %get-tuple-element.147), channel_id=1, source_target_pairs={{0,4},{4,8},{8,12},{1,5},{5,9},{9,13},{2,6},{6,10},{10,14},{3,7},{... | collective-permute-start | bytes 49160 | tf_op jit(solution)/shard_map/ppermute | solution.py:19
  122.3 11.8 %collective-permute-start.53 = (f32[2,2,1,1024]{3,2,1,0:T(1,128)S(1)}, f32[2,2,1,1024]{3,2,1,0:T(1,128)S(1)}, u32[]{:S(2)}, u32[]{:S(2)}) collective-permute-start(f32[2,2,1,1024]{3,2,1,0:T(1,128)S(1)} %get-tuple-element.106), channel_id=1, source_target_pairs={{4,0},{8,4},{12,8},{5,1},{9,5},{13,9},{6,2},{10,6},{14,10},{7,3},{... | collective-permute-start | bytes 49160 | tf_op jit(solution)/shard_map/ppermute | solution.py:21
  128.8 11.0 %collective-permute-start.11 = (f32[2,2,1,1024]{3,2,1,0:T(1,128)S(1)}, f32[2,2,1,1024]{3,2,1,0:T(1,128)S(1)}, u32[]{:S(2)}, u32[]{:S(2)}) collective-permute-start(f32[2,2,1,1024]{3,2,1,0:T(1,128)S(1)} %get-tuple-element.146), channel_id=1, source_target_pairs={{4,0},{8,4},{12,8},{5,1},{9,5},{13,9},{6,2},{10,6},{14,10},{7,3},{... | collective-permute-start | bytes 49160 | tf_op jit(solution)/shard_map/ppermute | solution.py:21
  134.5 11.0 %collective-permute-start.55 = (f32[2,2,1,1024]{3,2,1,0:T(1,128)S(1)}, f32[2,2,1,1024]{3,2,1,0:T(1,128)S(1)}, u32[]{:S(2)}, u32[]{:S(2)}) collective-permute-start(f32[2,2,1,1024]{3,2,1,0:T(1,128)S(1)} %get-tuple-element.104), channel_id=1, source_target_pairs={{4,0},{8,4},{12,8},{5,1},{9,5},{13,9},{6,2},{10,6},{14,10},{7,3},{... | collective-permute-start | bytes 49160 | tf_op jit(solution)/shard_map/ppermute | solution.py:21
  160.1 11.0 %collective-permute-start.57 = (f32[2,2,1,1024]{3,2,1,0:T(1,128)S(1)}, f32[2,2,1,1024]{3,2,1,0:T(1,128)S(1)}, u32[]{:S(2)}, u32[]{:S(2)}) collective-permute-start(f32[2,2,1,1024]{3,2,1,0:T(1,128)S(1)} %get-tuple-element.102), channel_id=1, source_target_pairs={{4,0},{8,4},{12,8},{5,1},{9,5},{13,9},{6,2},{10,6},{14,10},{7,3},{... | collective-permute-start | bytes 49160 | tf_op jit(solution)/shard_map/ppermute | solution.py:21
  192.6 29.7 %collective-permute-start.27 = (f32[2,2,1,1024]{3,2,1,0:T(1,128)S(1)}, f32[2,2,1,1024]{3,2,1,0:T(1,128)S(1)}, u32[]{:S(2)}, u32[]{:S(2)}) collective-permute-start(f32[2,2,1,1024]{3,2,1,0:T(1,128)S(1)} %get-tuple-element.130), channel_id=1, source_target_pairs={{4,0},{8,4},{12,8},{5,1},{9,5},{13,9},{6,2},{10,6},{14,10},{7,3},{... | collective-permute-start | bytes 49160 | tf_op jit(solution)/shard_map/ppermute | solution.py:21
  193.9 28.4 %collective-permute-start.28 = (f32[2,2,1,1024]{3,2,1,0:T(1,128)S(1)}, f32[2,2,1,1024]{3,2,1,0:T(1,128)S(1)}, u32[]{:S(2)}, u32[]{:S(2)}) collective-permute-start(f32[2,2,1,1024]{3,2,1,0:T(1,128)S(1)} %get-tuple-element.129), channel_id=1, source_target_pairs={{0,4},{4,8},{8,12},{1,5},{5,9},{9,13},{2,6},{6,10},{10,14},{3,7},{... | collective-permute-start | bytes 49160 | tf_op jit(solution)/shard_map/ppermute | solution.py:19
  198.2 27.1 %collective-permute-start.87 = (f32[2,2,8,1024]{3,2,1,0:T(8,128)S(1)}, f32[2,2,8,1024]{3,2,1,0:T(8,128)S(1)}, u32[]{:S(2)}, u32[]{:S(2)}) collective-permute-start(f32[2,2,8,1024]{3,2,1,0:T(8,128)S(1)} %pad_maximum_fusion.117), channel_id=1, source_target_pairs={{16,0},{32,16},{48,32},{64,48},{80,64},{96,80},{112,96},{128,112},... | collective-permute-start | bytes 393224 | tf_op jit(solution)/shard_map/ppermute | solution.py:31
  269.7 14.5 %collective-permute-start.100 = (f32[2,2,1,1024]{3,2,1,0:T(1,128)S(1)}, f32[2,2,1,1024]{3,2,1,0:T(1,128)S(1)}, u32[]{:S(2)}, u32[]{:S(2)}) collective-permute-start(f32[2,2,1,1024]{3,2,1,0:T(1,128)S(1)} %get-tuple-element.56), channel_id=1, source_target_pairs={{4,0},{8,4},{12,8},{5,1},{9,5},{13,9},{6,2},{10,6},{14,10},{7,3},{... | collective-permute-start | bytes 49160 | tf_op jit(solution)/shard_map/ppermute | solution.py:21
  271.0 13.3 %collective-permute-start.101 = (f32[2,2,1,1024]{3,2,1,0:T(1,128)S(1)}, f32[2,2,1,1024]{3,2,1,0:T(1,128)S(1)}, u32[]{:S(2)}, u32[]{:S(2)}) collective-permute-start(f32[2,2,1,1024]{3,2,1,0:T(1,128)S(1)} %get-tuple-element.55), channel_id=1, source_target_pairs={{0,4},{4,8},{8,12},{1,5},{5,9},{9,13},{2,6},{6,10},{10,14},{3,7},{... | collective-permute-start | bytes 49160 | tf_op jit(solution)/shard_map/ppermute | solution.py:19
  275.2 11.0 %collective-permute-start.29 = (f32[2,2,8,1024]{3,2,1,0:T(8,128)}, f32[2,2,8,1024]{3,2,1,0:T(8,128)S(1)}, u32[]{:S(2)}, u32[]{:S(2)}) collective-permute-start(f32[2,2,8,1024]{3,2,1,0:T(8,128)} %get-tuple-element.70), channel_id=1, source_target_pairs={{0,16},{16,32},{32,48},{48,64},{64,80},{80,96},{96,112},{112,128},... | collective-permute-start | bytes 393224 | tf_op jit(solution)/shard_map/ppermute | solution.py:31
  286.3 12.9 %collective-permute-start.59 = (f32[2,2,1,1024]{3,2,1,0:T(1,128)S(1)}, f32[2,2,1,1024]{3,2,1,0:T(1,128)S(1)}, u32[]{:S(2)}, u32[]{:S(2)}) collective-permute-start(f32[2,2,1,1024]{3,2,1,0:T(1,128)S(1)} %get-tuple-element.100), channel_id=1, source_target_pairs={{4,0},{8,4},{12,8},{5,1},{9,5},{13,9},{6,2},{10,6},{14,10},{7,3},{... | collective-permute-start | bytes 49160 | tf_op jit(solution)/shard_map/ppermute | solution.py:21
  287.6 11.6 %collective-permute-start.60 = (f32[2,2,1,1024]{3,2,1,0:T(1,128)S(1)}, f32[2,2,1,1024]{3,2,1,0:T(1,128)S(1)}, u32[]{:S(2)}, u32[]{:S(2)}) collective-permute-start(f32[2,2,1,1024]{3,2,1,0:T(1,128)S(1)} %get-tuple-element.99), channel_id=1, source_target_pairs={{0,4},{4,8},{8,12},{1,5},{5,9},{9,13},{2,6},{6,10},{10,14},{3,7},{... | collective-permute-start | bytes 49160 | tf_op jit(solution)/shard_map/ppermute | solution.py:19
  292.8 12.1 %collective-permute-start.102 = (f32[2,2,1,1024]{3,2,1,0:T(1,128)S(1)}, f32[2,2,1,1024]{3,2,1,0:T(1,128)S(1)}, u32[]{:S(2)}, u32[]{:S(2)}) collective-permute-start(f32[2,2,1,1024]{3,2,1,0:T(1,128)S(1)} %get-tuple-element.52), channel_id=1, source_target_pairs={{4,0},{8,4},{12,8},{5,1},{9,5},{13,9},{6,2},{10,6},{14,10},{7,3},{... | collective-permute-start | bytes 49160 | tf_op jit(solution)/shard_map/ppermute | solution.py:21
  311.0 11.0 %collective-permute-start.63 = (f32[2,2,1,1024]{3,2,1,0:T(1,128)S(1)}, f32[2,2,1,1024]{3,2,1,0:T(1,128)S(1)}, u32[]{:S(2)}, u32[]{:S(2)}) collective-permute-start(f32[2,2,1,1024]{3,2,1,0:T(1,128)S(1)} %get-tuple-element.96), channel_id=1, source_target_pairs={{4,0},{8,4},{12,8},{5,1},{9,5},{13,9},{6,2},{10,6},{14,10},{7,3},{... | collective-permute-start | bytes 49160 | tf_op jit(solution)/shard_map/ppermute | solution.py:21
  316.7 11.0 %collective-permute-start.106 = (f32[2,2,1,1024]{3,2,1,0:T(1,128)S(1)}, f32[2,2,1,1024]{3,2,1,0:T(1,128)S(1)}, u32[]{:S(2)}, u32[]{:S(2)}) collective-permute-start(f32[2,2,1,1024]{3,2,1,0:T(1,128)S(1)} %get-tuple-element.48), channel_id=1, source_target_pairs={{4,0},{8,4},{12,8},{5,1},{9,5},{13,9},{6,2},{10,6},{14,10},{7,3},{... | collective-permute-start | bytes 49160 | tf_op jit(solution)/shard_map/ppermute | solution.py:21
  322.4 11.0 %collective-permute-start.65 = (f32[2,2,1,1024]{3,2,1,0:T(1,128)S(1)}, f32[2,2,1,1024]{3,2,1,0:T(1,128)S(1)}, u32[]{:S(2)}, u32[]{:S(2)}) collective-permute-start(f32[2,2,1,1024]{3,2,1,0:T(1,128)S(1)} %get-tuple-element.94), channel_id=1, source_target_pairs={{4,0},{8,4},{12,8},{5,1},{9,5},{13,9},{6,2},{10,6},{14,10},{7,3},{... | collective-permute-start | bytes 49160 | tf_op jit(solution)/shard_map/ppermute | solution.py:21
  345.2 11.0 %collective-permute-start.69 = (f32[2,2,1,1024]{3,2,1,0:T(1,128)S(1)}, f32[2,2,1,1024]{3,2,1,0:T(1,128)S(1)}, u32[]{:S(2)}, u32[]{:S(2)}) collective-permute-start(f32[2,2,1,1024]{3,2,1,0:T(1,128)S(1)} %get-tuple-element.90), channel_id=1, source_target_pairs={{4,0},{8,4},{12,8},{5,1},{9,5},{13,9},{6,2},{10,6},{14,10},{7,3},{... | collective-permute-start | bytes 49160 | tf_op jit(solution)/shard_map/ppermute | solution.py:21
  (97 other events, 795.3 us)
Sparse Core Ops, SparseCore 0:
  416.9 80.1 all-reduce.58
where the time goes:
time: 511 us; the launch traced here: 505 us
  starting transfers between devices  346 us (68%)
  waiting for transfers between devices  106 us (21%)
  other arithmetic  30 us (6%)
  between operations  16.7 us (3%)
    ppermute x56, starting transfers between devices, extended(): lax.ppermute(tail, axis, [(i, (i + 1) % count) for i in range(ends)])  236 us
    psum x1, waiting for transfers between devices, local(): totals = lax.psum((correlation, illumination), 'freq')  78.9 us
    ppermute x56, starting transfers between devices, extended(): lax.ppermute(head, axis, [((i + 1) % count, i) for i in range(ends)])  72.4 us
    ppermute x4, starting transfers between devices, passed_along(): return lax.ppermute(block, axis, route)  37.7 us
    ppermute x56, waiting for transfers between devices, extended(): lax.ppermute(tail, axis, [(i, (i + 1) % count) for i in range(ends)])  15.1 us
    concatenate x56, other arithmetic, extended(): jnp.concatenate([lax.ppermute(tail, axis, [(i, (i + 1) % count) for i in...  12.6 us
    ppermute x4, waiting for transfers between devices, passed_along(): return lax.ppermute(block, axis, route)  11.9 us
  transfers between devices with their start and end apart: 117, of which 27 were waited for; matrix products, arithmetic and copies ran while one was open for 4% of the time, Pallas kernels for 0%

commit v1 on v0

v1 whole, which is shorter than its diff:
```python
import jax
import jax.numpy as jnp
from jax import lax
from jax.experimental import pallas as pl
from jax.experimental.pallas import tpu as pltpu
from jax.sharding import PartitionSpec as P

TICKS = 2
TERMS = 8
CLASSES = 64
LANES = 128
ROWS = 8
WIDE = 5
HALF = 4
FOLD = 4
TILE = (ROWS, LANES)
FIELD = (2, WIDE, FOLD) + TILE

VM = pl.BlockSpec(memory_space=pltpu.VMEM)
SM = pl.BlockSpec(memory_space=pltpu.SMEM)


def call(body, outs, scratch, limit, *args):
    many = isinstance(outs, (list, tuple)) and isinstance(outs[0], (list, tuple))
    shapes = [jax.ShapeDtypeStruct(s, jnp.float32) for s in outs] if many else jax.ShapeDtypeStruct(outs, jnp.float32)
    return pl.pallas_call(
        body,
        out_shape=shapes,
        in_specs=[SM if a.dtype == jnp.int32 and a.ndim == 1 else VM for a in args],
        out_specs=[VM] * len(outs) if many else VM,
        scratch_shapes=[pltpu.VMEM(s, jnp.float32) for s in scratch],
        compiler_params=pltpu.CompilerParams(vmem_limit_bytes=limit),
    )(*args)


def columns(tile):
    return slice(tile * LANES, (tile + 1) * LANES)


def pack_kernel(info, down, up, reflect, mask, classes, from_core, from_far, send):
    even = info[0] == 0
    for tile in range(2 * HALF):
        at = columns(tile)
        c = [reflect[lv, :, at] * mask[lv, :, at].astype(jnp.float32) for lv in range(2)]
        cls = [classes[lv, :, at].astype(jnp.float32) for lv in range(2)]
        places = [(h, tile - 3 * h) for h in range(2) if 0 <= tile - 3 * h < WIDE]
        for f in range(2):
            values = []
            for r in range(2):
                other = up if r == 0 else down
                for p in range(2):
                    a, b = from_core[p, f, :, at], from_far[p, f, :, at]
                    entry = jnp.where(even, b, a) if r == 0 else jnp.where(even, a, b)
                    values.append(entry + c[r] * other[r, p, f, :, at])
                for p in range(2):
                    values.append(c[1 - r] * other[1 - r, p, f, :, at])
            values += c + cls
            for h, j in places:
                for v, value in enumerate(values):
                    send[2 * h + f, v, j] = value


def filtered(read, write, level, table, terms, total):
    lane = lax.broadcasted_iota(jnp.int32, TILE, 1)
    sub = lax.broadcasted_iota(jnp.int32, TILE, 0)
    first_lane, last_lane = lane == 0, lane == LANES - 1
    first_sub, last_sub = sub == 0, sub == ROWS - 1
    spots = [(i, j) for i in range(FOLD) for j in range(WIDE)]

    def gather(order, i, j, real, imag):
        cr, ci = table[level, order, 0, j, i], table[level, order, 1, j, i]
        return cr * real - ci * imag, cr * imag + ci * real

    for i, j in spots:
        real, imag = read(0, j, i), read(1, j, i)
        terms[0, 0, j, i], terms[0, 1, j, i] = real, imag
        total[0, j, i], total[1, j, i] = gather(0, i, j, real, imag)
    for order in range(1, TERMS):
        now, before, new = (order - 1) % 3, (order - 2) % 3, order % 3
        for i in range(FOLD):
            made = []
            for p in range(2):
                here = [terms[now, p, j, i] for j in range(WIDE)]
                ahead = [pltpu.roll(x, 1, 1) for x in here]
                behind = [pltpu.roll(x, LANES - 1, 1) for x in here]
                row = []
                for j in range(WIDE):
                    west = jnp.where(first_lane, ahead[j - 1] if j else 0.0, ahead[j])
                    east = jnp.where(last_lane, behind[j + 1] if j + 1 < WIDE else 0.0, behind[j])
                    if i:
                        north = terms[now, p, j, i - 1]
                    else:
                        north = jnp.where(first_sub, 0.0, pltpu.roll(terms[now, p, j, FOLD - 1], 1, 0))
                    if i + 1 < FOLD:
                        south = terms[now, p, j, i + 1]
                    else:
                        south = jnp.where(last_sub, 0.0, pltpu.roll(terms[now, p, j, 0], ROWS - 1, 0))
                    around = (south + north) + (east + west)
                    if order == 1:
                        term = around * 0.25
                    else:
                        term = around * 0.5 - terms[before, p, j, i]
                    row.append(term)
                    if order + 1 < TERMS:
                        terms[new, p, j, i] = term
                made.append(row)
            for j in range(WIDE):
                dr, di = gather(order, i, j, made[0][j], made[1][j])
                real, imag = total[0, j, i] + dr, total[1, j, i] + di
                if order + 1 < TERMS:
                    total[0, j, i], total[1, j, i] = real, imag
                else:
                    write(0, j, i, real)
                    write(1, j, i, imag)


def first_kernel(info, recv, coeffs, state, to_core, to_far, coupling, table, rows, terms, total):
    f = info[1]
    for v in range(12):
        for j in range(WIDE):
            for s in range(FOLD):
                rows[v, j, s * ROWS : (s + 1) * ROWS, :] = recv[s, v, j]

    def folded(v, j, i):
        return rows[v, j, pl.ds(i, ROWS, stride=FOLD), :]

    for lv in range(2):
        for j in range(WIDE):
            for i in range(FOLD):
                coupling[lv, j, i] = folded(8 + lv, j, i)

    def build(order, carry):
        for p in range(2):
            lookup = jnp.broadcast_to(coeffs[f, p, pl.ds(order, 1), :], TILE)
            for lv in range(2):
                for j in range(WIDE):
                    for i in range(FOLD):
                        cls = folded(10 + lv, j, i).astype(jnp.int32)
                        table[lv, order, p, j, i] = jnp.take_along_axis(lookup, cls, axis=1, mode="promise_in_bounds")
        return carry

    lax.fori_loop(0, TERMS, build, 0)

    def sweep(r, carry):
        start, end = r, 1 - r

        def write_start(p, j, i, x):
            state[r, start, p, j, i] = x

        def write_end(p, j, i, x):
            state[r, end, p, j, i] = x

        filtered(lambda p, j, i: folded(4 * r + p, j, i), write_start, start, table, terms, total)
        filtered(
            lambda p, j, i: state[r, start, p, j, i] + folded(4 * r + 2 + p, j, i),
            write_end, end, table, terms, total,
        )
        return carry

    lax.fori_loop(0, 2, sweep, 0)
    even = info[0] == 0

    @pl.when(even)
    def _():
        to_core[...] = state[0, 1]
        to_far[...] = state[1, 0]

    @pl.when(jnp.logical_not(even))
    def _():
        to_core[...] = state[1, 0]
        to_far[...] = state[0, 1]


def second_kernel(info, from_core, from_far, state, coupling, table, send, result, rows, terms, total):
    parity, h = info[0], info[2]

    def sweep(r, carry):
        start, end = r, 1 - r
        core = parity + r == 1

        def read_start(p, j, i):
            entry = jnp.where(core, from_core[p, j, i], from_far[p, j, i])
            return entry + coupling[start, j, i] * state[1 - r, start, p, j, i]

        def read_end(p, j, i):
            return result[p, j, i] + coupling[end, j, i] * state[1 - r, end, p, j, i]

        def write(p, j, i, x):
            result[p, j, i] = x
            rows[p, j, pl.ds(i, ROWS, stride=FOLD), :] = x

        def put(level):
            for p in range(2):
                for j in range(HALF):
                    for s in range(FOLD):
                        send[s, 2 * r + level, p, j] = rows[p, h + j, s * ROWS : (s + 1) * ROWS, :]

        filtered(read_start, write, start, table, terms, total)
        put(start)
        filtered(read_end, write, end, table, terms, total)
        put(end)
        return carry

    lax.fori_loop(0, 2, sweep, 0)


def unpack_kernel(recv, down, up, sums):
    for lv in range(2):
        for h in range(2):
            for j in range(HALF):
                tile = HALF * h + j
                at = columns(tile)
                corr = illum = None
                for f in range(2):
                    s = 2 * h + f
                    d = [recv[s, lv, p, j] for p in range(2)]
                    u = [recv[s, 2 + lv, p, j] for p in range(2)]
                    for p in range(2):
                        down[lv, p, f, :, at] = d[p]
                        up[lv, p, f, :, at] = u[p]
                    one, two = d[0] * u[0] + d[1] * u[1], d[0] * d[0] + d[1] * d[1]
                    corr = one if corr is None else corr + one
                    illum = two if illum is None else illum + two
                sums[tile // 2, 0, lv, tile % 2] = corr
                sums[tile // 2, 1, lv, tile % 2] = illum


def image_kernel(recv, image):
    for lv in range(2):
        for t in range(2):
            corr = (recv[0, 0, lv, t] + recv[1, 0, lv, t]) + (recv[2, 0, lv, t] + recv[3, 0, lv, t])
            illum = (recv[0, 1, lv, t] + recv[1, 1, lv, t]) + (recv[2, 1, lv, t] + recv[3, 1, lv, t])
            image[lv, :, columns(t)] = corr / (1.0 + illum)


def local(down_state, up_state, reflect, layer_mask, classes, coeffs):
    depths = lax.axis_size("depth")
    position = lax.axis_index("depth")
    strip = lax.axis_index("strip")
    even = position % 2 == 0
    info = jnp.stack([position % 2, strip % 2, strip // 2]).astype(jnp.int32)
    pairs = [(i, i ^ 1) for i in range(depths)]
    far = [q for i in range(1, depths - 1, 2) for q in ((i, i + 1), (i + 1, i))]

    def crossed(to_core, to_far):
        return lax.ppermute(to_core, "depth", pairs), lax.ppermute(to_far, "depth", far)

    lookup = jnp.pad(jnp.transpose(coeffs, (2, 1, 3, 0)), ((0, 0), (0, 0), (0, 0), (0, LANES - CLASSES)))
    low, high = down_state[1], up_state[0]
    from_core, from_far = crossed(jnp.where(even, low, high), jnp.where(even, high, low))
    send = call(
        pack_kernel, (FOLD, 12, WIDE) + TILE, [], 16 << 20,
        info, down_state, up_state, reflect, layer_mask, classes, from_core, from_far,
    )
    recv = lax.all_to_all(send, "strip", 0, 0)
    work = [(3,) + FIELD, FIELD]
    state, to_core, to_far, coupling, table = call(
        first_kernel,
        [(2, 2) + FIELD, FIELD, FIELD, (2, WIDE, FOLD) + TILE, (2, TERMS) + FIELD],
        [(12, WIDE, FOLD * ROWS, LANES)] + work, 24 << 20,
        info, recv, lookup,
    )
    from_core, from_far = crossed(to_core, to_far)
    send = call(
        second_kernel, (FOLD, 4, 2, HALF) + TILE,
        [FIELD, (2, WIDE, FOLD * ROWS, LANES)] + work, 24 << 20,
        info, from_core, from_far, state, coupling, table,
    )
    recv = lax.all_to_all(send, "strip", 0, 0)
    whole = down_state.shape
    down, up, sums = call(unpack_kernel, [whole, whole, (4, 2, 2, 2) + TILE], [], 16 << 20, recv)
    sums = lax.all_to_all(sums, "freq", 0, 0)
    image = call(image_kernel, (2, ROWS, 2 * LANES), [], 4 << 20, sums)
    return down, up, image


def solution(mesh):
    placed = (
        P("depth", None, "freq", "strip", None),
        P("depth", None, "freq", "strip", None),
        P("depth", "strip", None),
        P("depth", "strip", None),
        P("depth", "strip", None),
        P(None, None, "freq", None),
    )
    return jax.shard_map(
        local,
        mesh=mesh,
        in_specs=placed,
        out_specs=(
            P("depth", None, "freq", "strip", None),
            P("depth", None, "freq", "strip", None),
            P("depth", "strip", "freq"),
        ),
        check_vma=False,
    )
```

time: 511 us -> 101 us (0.20); the launches traced: 505 us -> 100 us
  starting transfers between devices: 346 us -> 22.9 us
  waiting for transfers between devices: 106 us -> 38.8 us
  other arithmetic: 30 us -> 1.07 us
  blocking collectives: 0 us -> 20.2 us
  between operations: 16.7 us -> 0.74 us
  Pallas kernels: 0 us -> 12.3 us
    ppermute x116 -> x4, starting transfers between devices: 346 us -> 15.8 us  [the longest x2 11.9 us: crossed(): lax.ppermute(to_far, 'depth', far)]
    psum x1 -> x0, waiting for transfers between devices: 78.9 us -> none  [local(): totals = lax.psum((correlation, illumination), 'freq')]
    all_to_all x0 -> x1, waiting for transfers between devices: none -> 23.9 us  [local(): recv = lax.all_to_all(send, 'strip', 0, 0)]
    all_to_all x0 -> x2, blocking collectives: none -> 20.2 us  [the longest x1 11.5 us: local(): recv = lax.all_to_all(send, 'strip', 0, 0)]
    concatenate x56 -> x0, other arithmetic: 12.6 us -> none  [extended(): jnp.concatenate([lax.ppermute(tail, axis, [(i, (i + 1) % count) for i in...]
    pallas_call x0 -> x5, Pallas kernels: none -> 12.3 us  [call(): pl.pallas_call(body, out_shape=shapes, in_specs=[SM if a.dtype == jnp.int...]
    ppermute x116 -> x4, waiting for transfers between devices: 27.1 us -> 14.9 us  [the longest x2 14.9 us: crossed(): lax.ppermute(to_far, 'depth', far)]
    all_to_all x0 -> x1, starting transfers between devices: none -> 7.12 us  [local(): recv = lax.all_to_all(send, 'strip', 0, 0)]
  transfers between devices with their start and end apart: 117 -> 5, of which waited for: 27 -> 3; matrix products, arithmetic and copies ran while one was open for 4% -> 0% of each run, Pallas kernels for 0% -> 0%
where the time goes in v1:
time: 101 us; the launch traced here: 100 us
  waiting for transfers between devices  38.8 us (38%)
  starting transfers between devices  22.9 us (23%)
  blocking collectives  20.2 us (20%)
  Pallas kernels  12.3 us (12%)
  local copies, waits for them, and re-layouts  4.43 us (4%)
  other arithmetic  1.07 us (1%)
    all_to_all x1, waiting for transfers between devices, local(): recv = lax.all_to_all(send, 'strip', 0, 0)  23.9 us
    ppermute x2, waiting for transfers between devices, crossed(): lax.ppermute(to_far, 'depth', far)  14.9 us
    pallas_call x5, Pallas kernels, call(): pl.pallas_call(body, out_shape=shapes, in_specs=[SM if a.dtype == jnp.int...  12.3 us
    ppermute x2, starting transfers between devices, crossed(): lax.ppermute(to_far, 'depth', far)  11.9 us
    all_to_all x1, blocking collectives, local(): recv = lax.all_to_all(send, 'strip', 0, 0)  11.5 us
    all_to_all x1, blocking collectives, local(): sums = lax.all_to_all(sums, 'freq', 0, 0)  8.7 us
    all_to_all x1, starting transfers between devices, local(): recv = lax.all_to_all(send, 'strip', 0, 0)  7.12 us
    unnamed x13, local copies, waits for them, and re-layouts  4.42 us
  transfers between devices with their start and end apart: 5, of which 3 were waited for; matrix products, arithmetic and copies ran while one was open for 0% of the time, Pallas kernels for 0%

profile of v1, /device:TPU:25, one launch (start us, length us, event | category | flops | bytes accessed | tf_op | source)
XLA Modules:
  0.0 100.5 jit_solution(12834868309783913725)
XLA Ops:
  0.7 1.0 select_bitcast_fusion
  1.6 9.0 %collective-permute-start.1 = (f32[2,2,8,1024]{3,2,1,0:T(8,128)S(1)}, f32[2,2,8,1024]{3,2,1,0:T(8,128)S(1)}, u32[]{:S(2)}, u32[]{:S(2)}) collective-permute-start(f32[2,2,8,1024]{3,2,1,0:T(8,128)S(1)} %get-tuple-element.19), channel_id=1, source_target_pairs={{16,32},{32,16},{48,64},{64,48},{80,96},{96,80},{112,128},{128,112... | collective-permute-start | bytes 393224 | tf_op jit(solution)/shard_map/ppermute | solution.py:246
  10.7 1.9 %collective-permute-start = (f32[2,2,8,1024]{3,2,1,0:T(8,128)S(1)}, f32[2,2,8,1024]{3,2,1,0:T(8,128)S(1)}, u32[]{:S(2)}, u32[]{:S(2)}) collective-permute-start(f32[2,2,8,1024]{3,2,1,0:T(8,128)S(1)} %get-tuple-element.20), channel_id=1, source_target_pairs={{0,16},{16,0},{32,48},{48,32},{64,80},{80,64},{96,112},{112,96},{1... | collective-permute-start | bytes 393224 | tf_op jit(solution)/shard_map/ppermute | solution.py:246
  12.6 0.1 pad_add_fusion.info
  12.7 1.2 %collective-permute-done.1.from_far = f32[2,2,8,1024]{3,2,1,0:T(8,128)S(1)} collective-permute-done((f32[2,2,8,1024]{3,2,1,0:T(8,128)S(1)}, f32[2,2,8,1024]{3,2,1,0:T(8,128)S(1)}, u32[]{:S(2)}, u32[]{:S(2)}) %collective-permute-start.1) | collective-permute-done | bytes 131104 | tf_op jit(solution)/shard_map/ppermute | solution.py:246
  14.0 0.0 collective-permute-done.from_core
  14.0 0.9 copy-done
  14.9 0.9 copy-done.1
  15.9 0.8 copy-done.2
  16.7 0.8 copy-done.3
  17.6 0.8 copy-done.4
  18.4 1.6 %shard_map.85 = f32[4,12,5,8,128]{4,3,2,1,0:T(8,128)} custom-call(s32[3]{0:T(128)S(1)} %pad_add_fusion.info, f32[2,2,2,8,1024]{4,3,2,1,0:T(8,128)S(1)} %copy-done, f32[2,2,2,8,1024]{4,3,2,1,0:T(8,128)S(1)} %copy-done.1, f32[2,8,1024]{2,1,0:T(8,128)S(1)} %copy-done.2, s32[2,8,1024]{2,1,0:T(8,128)S(1)} %copy-done.3, s32[2,8,1024]{2,1,0:T(8,128)S(1)} %copy-done.4, ...), custom_call_target="tpu_custom_call" | custom-call | tf_op jit(solution)/shard_map/pallas_call | solution.py:26
  20.0 7.1 %all-to-all-start = ((f32[4,12,5,8,128]{4,3,2,1,0:T(8,128)}), f32[4,12,5,8,128]{4,3,2,1,0:T(8,128)S(1)}, u32[]{:S(2)}, u32[]{:S(2)}) async-start(f32[4,12,5,8,128]{4,3,2,1,0:T(8,128)} %shard_map.85), calls=%async_computation | async-start | bytes 1966080 | tf_op jit(solution)/shard_map/all_to_all | solution.py:255
  27.1 23.9 %all-to-all-done.recv = f32[4,12,5,8,128]{4,3,2,1,0:T(8,128)S(1)} async-done(((f32[4,12,5,8,128]{4,3,2,1,0:T(8,128)}), f32[4,12,5,8,128]{4,3,2,1,0:T(8,128)S(1)}, u32[]{:S(2)}, u32[]{:S(2)}) %all-to-all-start) | async-done | bytes 983072 | tf_op jit(solution)/shard_map/all_to_all | solution.py:255
  51.0 5.9 %shard_map.86 = (f32[2,2,2,5,4,8,128]{6,5,4,3,2,1,0:T(8,128)S(1)}, f32[2,5,4,8,128]{4,3,2,1,0:T(8,128)S(1)}, f32[2,5,4,8,128]{4,3,2,1,0:T(8,128)S(1)}, f32[2,5,4...) custom-call(s32[3]{0:T(128)S(1)} %pad_add_fusion.info, f32[4,12,5,8,128]{4,3,2,1,0:T(8,128)S(1)} %all-to-all-done.recv, ...), custom_call_target="tpu_custom_call" | custom-call | tf_op jit(solution)/shard_map/pallas_call | solution.py:26
  56.9 1.9 %collective-permute-start.2 = (f32[2,5,4,8,128]{4,3,2,1,0:T(8,128)S(1)}, f32[2,5,4,8,128]{4,3,2,1,0:T(8,128)S(1)}, u32[]{:S(2)}, u32[]{:S(2)}) collective-permute-start(f32[2,5,4,8,128]{4,3,2,1,0:T(8,128)S(1)} %get-tuple-element.11), channel_id=1, source_target_pairs={{0,16},{16,0},{32,48},{48,32},{64,80},{80,64},{96,112},{112,96},{1... | collective-permute-start | bytes 491528 | tf_op jit(solution)/shard_map/ppermute | solution.py:246
  58.8 2.9 %collective-permute-start.3 = (f32[2,5,4,8,128]{4,3,2,1,0:T(8,128)S(1)}, f32[2,5,4,8,128]{4,3,2,1,0:T(8,128)S(1)}, u32[]{:S(2)}, u32[]{:S(2)}) collective-permute-start(f32[2,5,4,8,128]{4,3,2,1,0:T(8,128)S(1)} %get-tuple-element.12), channel_id=1, source_target_pairs={{16,32},{32,16},{48,64},{64,48},{80,96},{96,80},{112,128},{128,112... | collective-permute-start | bytes 491528 | tf_op jit(solution)/shard_map/ppermute | solution.py:246
  61.7 0.0 collective-permute-done.2.from_core
  61.7 13.6 %collective-permute-done.3.from_far = f32[2,5,4,8,128]{4,3,2,1,0:T(8,128)S(1)} collective-permute-done((f32[2,5,4,8,128]{4,3,2,1,0:T(8,128)S(1)}, f32[2,5,4,8,128]{4,3,2,1,0:T(8,128)S(1)}, u32[]{:S(2)}, u32[]{:S(2)}) %collective-permute-start.3) | collective-permute-done | bytes 163872 | tf_op jit(solution)/shard_map/ppermute | solution.py:246
  75.4 3.4 %shard_map.87 = f32[4,4,2,4,8,128]{5,4,3,2,1,0:T(8,128)S(1)} custom-call(s32[3]{0:T(128)S(1)} %pad_add_fusion.info, f32[2,5,4,8,128]{4,3,2,1,0:T(8,128)S(1)} %collective-permute-done.2.from_core, f32[2,5,4,8,128]{4,3,2,1,0:T(8,128)S(1)} %collective-permute-done.3.from_far, f32[2,2,2,5,4,8,128]{6,5,4,3,2,1,0:T(8,128)S(1)} %get-tuple-element.13.state, ...), custom_call_target="tpu_custom_call" | custom-call | tf_op jit(solution)/shard_map/pallas_call | solution.py:26
  78.8 11.5 %all_to_all.15.recv = f32[4,4,2,4,8,128]{5,4,3,2,1,0:T(8,128)S(1)} all-to-all(f32[4,4,2,4,8,128]{5,4,3,2,1,0:T(8,128)S(1)} %shard_map.87), channel_id=1, replica_groups=mesh['depth'=32,'strip'=4,'freq'=4] {'strip'}, dimensions={0} | all-to-all | bytes 1048576 | tf_op jit(solution)/shard_map/all_to_all | solution.py:269
  90.3 0.8 shard_map.88
  91.2 8.7 %all_to_all.16.recv = f32[4,2,2,2,8,128]{5,4,3,2,1,0:T(8,128)S(1)} all-to-all(f32[4,2,2,2,8,128]{5,4,3,2,1,0:T(8,128)S(1)} %get-tuple-element.18), channel_id=1, replica_groups=mesh['depth'=32,'strip'=4,'freq'=4] {'freq'}, dimensions={0} | all-to-all | bytes 262144 | tf_op jit(solution)/shard_map/all_to_all | solution.py:272
  99.9 0.6 shard_map.89
  (9 shorter events, 0.0 us)
Async XLA Ops:
  0.6 26.5 %copy-start.5 = (f32[64,2,2,8]{0,3,2,1:T(8,128)S(1)}, f32[64,2,2,8]{0,3,2,1:T(8,128)}, u32[]{:S(2)}) copy-start(f32[64,2,2,8]{0,3,2,1:T(8,128)} %param.11) | copy-start | bytes 24580
  1.6 12.3 %collective-permute-start.1 = (f32[2,2,8,1024]{3,2,1,0:T(8,128)S(1)}, f32[2,2,8,1024]{3,2,1,0:T(8,128)S(1)}, u32[]{:S(2)}, u32[]{:S(2)}) collective-permute-start(f32[2,2,8,1024]{3,2,1,0:T(8,128)S(1)} %get-tuple-element.19), channel_id=1, source_target_pairs={{16,32},{32,16},{48,64},{64,48},{80,96},{96,80},{112,128},{128,112... | collective-permute-start | bytes 393224 | tf_op jit(solution)/shard_map/ppermute | solution.py:246
  10.7 3.3 %collective-permute-start = (f32[2,2,8,1024]{3,2,1,0:T(8,128)S(1)}, f32[2,2,8,1024]{3,2,1,0:T(8,128)S(1)}, u32[]{:S(2)}, u32[]{:S(2)}) collective-permute-start(f32[2,2,8,1024]{3,2,1,0:T(8,128)S(1)} %get-tuple-element.20), channel_id=1, source_target_pairs={{0,16},{16,0},{32,48},{48,32},{64,80},{80,64},{96,112},{112,96},{1... | collective-permute-start | bytes 393224 | tf_op jit(solution)/shard_map/ppermute | solution.py:246
  14.0 1.0 copy-start
  14.9 0.9 copy-start.1
  15.9 0.8 copy-start.2
  16.7 0.8 copy-start.3
  17.6 0.8 copy-start.4
  20.0 31.1 %all-to-all-start = ((f32[4,12,5,8,128]{4,3,2,1,0:T(8,128)}), f32[4,12,5,8,128]{4,3,2,1,0:T(8,128)S(1)}, u32[]{:S(2)}, u32[]{:S(2)}) async-start(f32[4,12,5,8,128]{4,3,2,1,0:T(8,128)} %shard_map.85), calls=%async_computation | async-start | bytes 1966080 | tf_op jit(solution)/shard_map/all_to_all | solution.py:255
  56.9 4.8 %collective-permute-start.2 = (f32[2,5,4,8,128]{4,3,2,1,0:T(8,128)S(1)}, f32[2,5,4,8,128]{4,3,2,1,0:T(8,128)S(1)}, u32[]{:S(2)}, u32[]{:S(2)}) collective-permute-start(f32[2,5,4,8,128]{4,3,2,1,0:T(8,128)S(1)} %get-tuple-element.11), channel_id=1, source_target_pairs={{0,16},{16,0},{32,48},{48,32},{64,80},{80,64},{96,112},{112,96},{1... | collective-permute-start | bytes 491528 | tf_op jit(solution)/shard_map/ppermute | solution.py:246
  58.8 16.5 %collective-permute-start.3 = (f32[2,5,4,8,128]{4,3,2,1,0:T(8,128)S(1)}, f32[2,5,4,8,128]{4,3,2,1,0:T(8,128)S(1)}, u32[]{:S(2)}, u32[]{:S(2)}) collective-permute-start(f32[2,5,4,8,128]{4,3,2,1,0:T(8,128)S(1)} %get-tuple-element.12), channel_id=1, source_target_pairs={{16,32},{32,16},{48,64},{64,48},{80,96},{96,80},{112,128},{128,112... | collective-permute-start | bytes 491528 | tf_op jit(solution)/shard_map/ppermute | solution.py:246

commit v2 on v1

v2 whole, which is shorter than its diff:
```python
import functools

import jax
import jax.numpy as jnp
from jax import lax
from jax.experimental import pallas as pl
from jax.experimental.pallas import tpu as pltpu
from jax.sharding import PartitionSpec as P


TERMS = 8
CLASSES = 64
LANES = 128
ROWS = 8
WIDE = 5
HALF = 4
FOLD = 4
VALUES = 12
EDGE = 32
PACK = LANES // EDGE
TILE = (ROWS, LANES)
FIELD = (2, WIDE, FOLD) + TILE

VM = pl.BlockSpec(memory_space=pltpu.VMEM)
SM = pl.BlockSpec(memory_space=pltpu.SMEM)
HB = pl.BlockSpec(memory_space=pltpu.HBM)


def call(body, outs, scratch, limit, *args, stay=0):
    many = isinstance(outs, (list, tuple)) and isinstance(outs[0], (list, tuple))
    shapes = [jax.ShapeDtypeStruct(s, jnp.float32) for s in outs] if many else jax.ShapeDtypeStruct(outs, jnp.float32)
    specs = [SM if n == 0 and a.dtype == jnp.int32 else HB if 1 <= n <= stay else VM for n, a in enumerate(args)]
    return pl.pallas_call(
        body,
        out_shape=shapes,
        in_specs=specs,
        out_specs=[VM] * len(outs) if many else VM,
        scratch_shapes=[pltpu.VMEM(s, jnp.float32) if isinstance(s, tuple) else s for s in scratch],
        compiler_params=pltpu.CompilerParams(vmem_limit_bytes=limit),
    )(*args)


def columns(tile):
    return slice(tile * LANES, (tile + 1) * LANES)


def pack_kernel(info, *refs):
    _, _, _, _, _, send, fields, reflects, masks, cells, sems = refs
    held = (fields.at[0], fields.at[1], reflects, masks, cells)
    copies = [pltpu.make_async_copy(a, b, sems.at[n]) for n, (a, b) in enumerate(zip(refs[:5], held))]
    for copy in copies:
        copy.start()
    for copy in copies:
        copy.wait()
    parity = info[0]
    lane = lax.broadcasted_iota(jnp.int32, TILE, 1)
    for tile in range(2 * HALF):
        at = columns(tile)
        shared = [reflects[lv, :, at] * masks[lv, :, at].astype(jnp.float32) for lv in range(2)]
        shared += [cells[lv, :, at].astype(jnp.float32) for lv in range(2)]
        h = tile // HALF
        for f in range(2):
            values = []
            for r in (1 - parity, parity):
                for level in (1 - r, r):
                    values += [fields[r, level, p, f, :, at] for p in range(2)]
            values += shared
            for v, value in enumerate(values):
                send[2 * h + f, HALF * v + tile % HALF] = value
            if tile in (HALF - 1, HALF):
                other = 1 - h
                from_lane = 0 if tile == HALF else LANES - EDGE
                for group in range(VALUES // PACK):
                    packed = None
                    for q in range(PACK):
                        shift = (EDGE * q - from_lane) % LANES
                        moved = values[PACK * group + q]
                        moved = pltpu.roll(moved, shift, 1) if shift else moved
                        packed = moved if packed is None else jnp.where(lane >= EDGE * q, moved, packed)
                    send[2 * other + f, HALF * VALUES + group] = packed


def fold_kernel(info, recv, first_end, first_start, second_end, second_start, coupling, cells, rows):
    h = info[2]
    lane = lax.broadcasted_iota(jnp.int32, TILE, 1)
    inside = jnp.where(h == 0, lane, LANES - 1 - lane) < EDGE
    for s in range(FOLD):
        at = slice(s * ROWS, (s + 1) * ROWS)
        for v in range(VALUES):
            for j in range(HALF):
                rows[v, h + j, at, :] = recv[s, HALF * v + j]
            packed = recv[s, HALF * VALUES + v // PACK]
            moved = pltpu.roll(packed, (LANES - EDGE * (v % PACK)) % LANES + (LANES - EDGE) * h, 1)
            rows[v, HALF * (1 - h), at, :] = jnp.where(inside, moved, 0.0)

    def folded(v, j, i):
        return rows[v, j, pl.ds(i, ROWS, stride=FOLD), :]

    for j in range(WIDE):
        for i in range(FOLD):
            for p in range(2):
                first_end[p, j, i] = folded(p, j, i)
                first_start[p, j, i] = folded(2 + p, j, i)
                second_end[p, j, i] = folded(4 + p, j, i)
                second_start[p, j, i] = folded(6 + p, j, i)
            for lv in range(2):
                coupling[lv, j, i] = folded(8 + lv, j, i)
                cells[lv, j, i] = folded(10 + lv, j, i)


def table_kernel(info, cells, coeffs, table):
    f = info[1]

    def build(order, carry):
        lookups = [jnp.broadcast_to(coeffs[f, p, pl.ds(order, 1), :], TILE) for p in range(2)]
        for lv in range(2):
            for j in range(WIDE):
                for i in range(FOLD):
                    cls = cells[lv, j, i].astype(jnp.int32)
                    for p in range(2):
                        table[lv, order, p, j, i] = jnp.take_along_axis(
                            lookups[p], cls, axis=1, mode="promise_in_bounds"
                        )
        return carry

    lax.fori_loop(0, TERMS, build, 0)


def filtered(read, write, level, table, terms, total):
    lane = lax.broadcasted_iota(jnp.int32, TILE, 1)
    sub = lax.broadcasted_iota(jnp.int32, TILE, 0)
    first_lane, last_lane = lane == 0, lane == LANES - 1
    first_sub, last_sub = sub == 0, sub == ROWS - 1
    spots = [(i, j) for i in range(FOLD) for j in range(WIDE)]

    def gather(order, i, j, real, imag):
        cr, ci = table[level, order, 0, j, i], table[level, order, 1, j, i]
        return cr * real - ci * imag, cr * imag + ci * real

    for i, j in spots:
        real, imag = read(0, j, i), read(1, j, i)
        terms[0, 0, j, i], terms[0, 1, j, i] = real, imag
        total[0, j, i], total[1, j, i] = gather(0, i, j, real, imag)
    for order in range(1, TERMS):
        now, before, new = (order - 1) % 3, (order - 2) % 3, order % 3
        for i in range(FOLD):
            made = []
            for p in range(2):
                here = [terms[now, p, j, i] for j in range(WIDE)]
                ahead = [pltpu.roll(x, 1, 1) for x in here]
                behind = [pltpu.roll(x, LANES - 1, 1) for x in here]
                row = []
                for j in range(WIDE):
                    west = jnp.where(first_lane, ahead[j - 1] if j else 0.0, ahead[j])
                    east = jnp.where(last_lane, behind[j + 1] if j + 1 < WIDE else 0.0, behind[j])
                    if i:
                        north = terms[now, p, j, i - 1]
                    else:
                        north = jnp.where(first_sub, 0.0, pltpu.roll(terms[now, p, j, FOLD - 1], 1, 0))
                    if i + 1 < FOLD:
                        south = terms[now, p, j, i + 1]
                    else:
                        south = jnp.where(last_sub, 0.0, pltpu.roll(terms[now, p, j, 0], ROWS - 1, 0))
                    around = (south + north) + (east + west)
                    if order == 1:
                        term = around * 0.25
                    else:
                        term = around * 0.5 - terms[before, p, j, i]
                    row.append(term)
                    if order + 1 < TERMS:
                        terms[new, p, j, i] = term
                made.append(row)
            for j in range(WIDE):
                dr, di = gather(order, i, j, made[0][j], made[1][j])
                real, imag = total[0, j, i] + dr, total[1, j, i] + di
                if order + 1 < TERMS:
                    total[0, j, i], total[1, j, i] = real, imag
                else:
                    write(0, j, i, real)
                    write(1, j, i, imag)


def direction(info, second):
    return info[0] if second else 1 - info[0]


def first_kernel(second, info, entry, start_other, end_other, coupling, table, *refs):
    start_out, end_out, terms, total = refs[-4:]
    r = direction(info, second)
    start, end = r, 1 - r

    def read_start(p, j, i):
        return entry[p, j, i] + coupling[start, j, i] * end_other[p, j, i]

    def read_end(p, j, i):
        return start_out[p, j, i] + coupling[end, j, i] * start_other[p, j, i]

    def write_start(p, j, i, x):
        start_out[p, j, i] = x

    def write_end(p, j, i, x):
        end_out[p, j, i] = x

    filtered(read_start, write_start, start, table, terms, total)
    filtered(read_end, write_end, end, table, terms, total)


def second_kernel(second, info, entry, start_other, end_other, coupling, table, *refs):
    if second:
        earlier, send, result, rows, terms, total = refs
    else:
        send, result, rows, terms, total = refs
    r, h = direction(info, second), info[2]
    start, end = r, 1 - r

    def read_start(p, j, i):
        return entry[p, j, i] + coupling[start, j, i] * end_other[p, j, i]

    def read_end(p, j, i):
        return result[p, j, i] + coupling[end, j, i] * start_other[p, j, i]

    def write(p, j, i, x):
        result[p, j, i] = x
        rows[p, j, pl.ds(i, ROWS, stride=FOLD), :] = x

    def put(level):
        for p in range(2):
            for j in range(HALF):
                for s in range(FOLD):
                    value = rows[p, h + j, s * ROWS : (s + 1) * ROWS, :]
                    if second:
                        send[s, 2 * r + level, p, j] = value
                    else:
                        send[s, level, p, j] = value

    filtered(read_start, write, start, table, terms, total)
    put(start)
    filtered(read_end, write, end, table, terms, total)
    put(end)
    if second:
        for s in range(FOLD):
            for level in range(2):
                for p in range(2):
                    for j in range(HALF):
                        send[s, 2 * (1 - r) + level, p, j] = earlier[s, level, p, j]


def sums_kernel(recv, sums):
    for lv in range(2):
        for tile in range(2 * HALF):
            h, j = tile // HALF, tile % HALF
            corr = illum = None
            for f in range(2):
                d = [recv[2 * h + f, lv, p, j] for p in range(2)]
                u = [recv[2 * h + f, 2 + lv, p, j] for p in range(2)]
                one, two = d[0] * u[0] + d[1] * u[1], d[0] * d[0] + d[1] * d[1]
                corr = one if corr is None else corr + one
                illum = two if illum is None else illum + two
            sums[tile // 2, 0, lv, tile % 2] = corr
            sums[tile // 2, 1, lv, tile % 2] = illum


def unpack_kernel(recv, down, up):
    for n, out in enumerate((down, up)):
        for lv in range(2):
            for p in range(2):
                for tile in range(2 * HALF):
                    for f in range(2):
                        out[lv, p, f, :, columns(tile)] = recv[2 * (tile // HALF) + f, 2 * n + lv, p, tile % HALF]


def image_kernel(recv, image):
    for lv in range(2):
        for t in range(2):
            corr = (recv[0, 0, lv, t] + recv[1, 0, lv, t]) + (recv[2, 0, lv, t] + recv[3, 0, lv, t])
            illum = (recv[0, 1, lv, t] + recv[1, 1, lv, t]) + (recv[2, 1, lv, t] + recv[3, 1, lv, t])
            image[lv, :, columns(t)] = corr / (1.0 + illum)


def local(down_state, up_state, reflect, layer_mask, classes, coeffs):
    depths = lax.axis_size("depth")
    position = lax.axis_index("depth")
    strip = lax.axis_index("strip")
    info = jnp.stack([position % 2, strip % 2, strip // 2]).astype(jnp.int32)
    pairs = [(i, i ^ 1) for i in range(depths)]
    far = [q for i in range(1, depths - 1, 2) for q in ((i, i + 1), (i + 1, i))]
    lookup = jnp.pad(jnp.transpose(coeffs, (2, 1, 3, 0)), ((0, 0), (0, 0), (0, 0), (0, LANES - CLASSES)))
    sources = (down_state, up_state, reflect, layer_mask, classes)
    held = [pltpu.VMEM(a.shape, a.dtype) for a in (jax.ShapeDtypeStruct((2,) + up_state.shape, jnp.float32),) + sources[2:]]
    send = call(
        pack_kernel, (FOLD, HALF * VALUES + VALUES // PACK) + TILE,
        held + [pltpu.SemaphoreType.DMA((5,))], 60 * 1024 * 1024, info, *sources, stay=5,
    )
    recv = lax.all_to_all(send, "strip", 0, 0)
    folded = (2, WIDE, FOLD) + TILE
    end1, start1, end2, start2, coupling, cells = call(
        fold_kernel, [FIELD] * 4 + [folded] * 2, [(VALUES, WIDE, FOLD * ROWS, LANES)], 16 << 20, info, recv
    )
    from_far = lax.ppermute(end1, "depth", far)
    from_core = lax.ppermute(end2, "depth", pairs)
    table = call(table_kernel, (2, TERMS) + FIELD, [], 16 << 20, info, cells, lookup)
    work = [(3,) + FIELD, FIELD]

    def first(second, entry, other, *after):
        body = functools.partial(first_kernel, second)
        return call(body, [FIELD, FIELD], work, 16 << 20, info, entry, *other, coupling, table, *after)

    def last(second, entry, other, *earlier):
        body = functools.partial(second_kernel, second)
        out = (FOLD, 4 if second else 2, 2, HALF) + TILE
        scratch = [FIELD, (2, WIDE, FOLD * ROWS, LANES)] + work
        return call(body, out, scratch, 16 << 20, info, entry, *other, coupling, table, *earlier)

    one = first(False, from_core, (start2, end2))
    ahead = lax.ppermute(one[1], "depth", far)
    two = first(True, from_far, (start1, end1), one[0])
    from_core = lax.ppermute(two[1], "depth", pairs)
    part = last(False, from_core, two)
    send = last(True, ahead, one, part)
    recv = lax.all_to_all(send, "strip", 0, 0)
    sums = call(sums_kernel, (4, 2, 2, 2) + TILE, [], 16 << 20, recv)
    sums = lax.all_to_all(sums, "freq", 0, 0)
    down, up = call(unpack_kernel, [down_state.shape, up_state.shape], [], 16 << 20, recv)
    image = call(image_kernel, (2, ROWS, 2 * LANES), [], 4 << 20, sums)
    return down, up, image


def solution(mesh):
    placed = (
        P("depth", None, "freq", "strip", None),
        P("depth", None, "freq", "strip", None),
        P("depth", "strip", None),
        P("depth", "strip", None),
        P("depth", "strip", None),
        P(None, None, "freq", None),
    )
    return jax.shard_map(
        local,
        mesh=mesh,
        in_specs=placed,
        out_specs=(
            P("depth", None, "freq", "strip", None),
            P("depth", None, "freq", "strip", None),
            P("depth", "strip", "freq"),
        ),
        check_vma=False,
    )
```

time: 101 us -> 97.3 us (0.963)
  the two profiles are of different devices: /device:TPU:25 before, /device:TPU:128 now
where the time goes in v2:
time: 97.3 us; the launch traced here: 96.9 us
  blocking collectives  46.3 us (48%)
  starting transfers between devices  19.4 us (20%)
  Pallas kernels  16 us (16%)
  waiting for transfers between devices  13.7 us (14%)
    all_to_all x2, blocking collectives, local(): recv = lax.all_to_all(send, 'strip', 0, 0)  46.3 us
    pallas_call x10, Pallas kernels, call(): pl.pallas_call(body, out_shape=shapes, in_specs=specs, out_specs=[VM] * l...  16 us
    ppermute x1, starting transfers between devices, local(): ahead = lax.ppermute(one[1], 'depth', far)  8.08 us
    all_to_all x1, waiting for transfers between devices, local(): sums = lax.all_to_all(sums, 'freq', 0, 0)  5.15 us
    ppermute x1, waiting for transfers between devices, local(): from_far = lax.ppermute(end1, 'depth', far)  5.14 us
    all_to_all x1, starting transfers between devices, local(): sums = lax.all_to_all(sums, 'freq', 0, 0)  4.29 us
    ppermute x1, waiting for transfers between devices, local(): ahead = lax.ppermute(one[1], 'depth', far)  3.36 us
    ppermute x1, starting transfers between devices, local(): from_far = lax.ppermute(end1, 'depth', far)  3.21 us
  transfers between devices with their start and end apart: 5, of which 3 were waited for; matrix products, arithmetic and copies ran while one was open for 0% of the time, Pallas kernels for 7%

profile of v2, /device:TPU:128, one launch (start us, length us, event | category | flops | bytes accessed | tf_op | source)
XLA Modules:
  0.0 96.9 jit_solution(102481698481179768)
XLA Ops:
  0.6 0.0 copy-start.1
  0.7 0.7 pad_add_fusion.info
  1.3 2.9 %shard_map.85 = f32[4,51,8,128]{3,2,1,0:T(8,128)} custom-call(s32[3]{0:T(128)} %pad_add_fusion.info, f32[2,2,2,8,1024]{4,3,2,1,0:T(8,128)} %refs_0_.1, f32[2,2,2,8,1024]{4,3,2,1,0:T(8,128)} %refs_1_.1, f32[2,8,1024]{2,1,0:T(8,128)} %refs_2_.1, s32[2,8,1024]{2,1,0:T(8,128)} %refs_3_.1, s32[2,8,1024]{2,1,0:T(8,128)} %refs_4_.1), custom_call_target="tpu_custom_call" | custom-call | tf_op jit(solution)/shard_map/pallas_call | solution.py:33
  4.2 27.1 %all_to_all.15.recv = f32[4,51,8,128]{3,2,1,0:T(8,128)S(1)} all-to-all(f32[4,51,8,128]{3,2,1,0:T(8,128)} %shard_map.85), channel_id=1, replica_groups=mesh['depth'=32,'strip'=4,'freq'=4] {'strip'}, dimensions={0} | all-to-all | bytes 1671168 | tf_op jit(solution)/shard_map/all_to_all | solution.py:294
  31.3 0.8 shard_map.86
  32.1 1.9 %collective-permute-start = (f32[2,5,4,8,128]{4,3,2,1,0:T(8,128)S(1)}, f32[2,5,4,8,128]{4,3,2,1,0:T(8,128)S(1)}, u32[]{:S(2)}, u32[]{:S(2)}) collective-permute-start(f32[2,5,4,8,128]{4,3,2,1,0:T(8,128)S(1)} %get-tuple-element.15.end_other), channel_id=1, source_target_pairs={{0,16},{16,0},{32,48},{48,32},{64,80},{80,64},{96,112},{112,96},{1... | collective-permute-start | bytes 491528 | tf_op jit(solution)/shard_map/ppermute | solution.py:300
  34.1 3.2 %collective-permute-start.2 = (f32[2,5,4,8,128]{4,3,2,1,0:T(8,128)S(1)}, f32[2,5,4,8,128]{4,3,2,1,0:T(8,128)S(1)}, u32[]{:S(2)}, u32[]{:S(2)}) collective-permute-start(f32[2,5,4,8,128]{4,3,2,1,0:T(8,128)S(1)} %get-tuple-element.21.end_other), channel_id=1, source_target_pairs={{16,32},{32,16},{48,64},{64,48},{80,96},{96,80},{112,128},{128,112... | collective-permute-start | bytes 491528 | tf_op jit(solution)/shard_map/ppermute | solution.py:299
  37.3 2.6 %shard_map.87.table = f32[2,8,2,5,4,8,128]{6,5,4,3,2,1,0:T(8,128)S(1)} custom-call(s32[3]{0:T(128)S(1)} %copy-done, f32[2,5,4,8,128]{4,3,2,1,0:T(8,128)S(1)} %get-tuple-element.18.cells, f32[2,2,8,128]{3,2,1,0:T(8,128)S(1)} %pad.4.coeffs), custom_call_target="tpu_custom_call" | custom-call | tf_op jit(solution)/shard_map/pallas_call | solution.py:33
  39.9 0.0 collective-permute-done.entry
  39.9 1.9 %shard_map.88 = (f32[2,5,4,8,128]{4,3,2,1,0:T(8,128)S(1)}, f32[2,5,4,8,128]{4,3,2,1,0:T(8,128)S(1)}) custom-call(s32[3]{0:T(128)S(1)} %copy-done, f32[2,5,4,8,128]{4,3,2,1,0:T(8,128)S(1)} %collective-permute-done.entry, f32[2,5,4,8,128]{4,3,2,1,0:T(8,128)S(1)} %get-tuple-element.16.start_other, f32[2,5,4,8,128]{4,3,2,1,0:T(8,128)S(1)} %get-tuple-element.15.end_other, ...), custom_call_target="tpu_custom_call" | custom-call | tf_op jit(solution)/shard_map/pallas_call | solution.py:33
  41.8 5.1 %collective-permute-done.2.entry = f32[2,5,4,8,128]{4,3,2,1,0:T(8,128)S(1)} collective-permute-done((f32[2,5,4,8,128]{4,3,2,1,0:T(8,128)S(1)}, f32[2,5,4,8,128]{4,3,2,1,0:T(8,128)S(1)}, u32[]{:S(2)}, u32[]{:S(2)}) %collective-permute-start.2) | collective-permute-done | bytes 163872 | tf_op jit(solution)/shard_map/ppermute | solution.py:299
  47.0 1.9 %shard_map.89 = (f32[2,5,4,8,128]{4,3,2,1,0:T(8,128)S(1)}, f32[2,5,4,8,128]{4,3,2,1,0:T(8,128)S(1)}) custom-call(s32[3]{0:T(128)S(1)} %copy-done, f32[2,5,4,8,128]{4,3,2,1,0:T(8,128)S(1)} %collective-permute-done.2.entry, f32[2,5,4,8,128]{4,3,2,1,0:T(8,128)S(1)} %get-tuple-element.22.start_other, f32[2,5,4,8,128]{4,3,2,1,0:T(8,128)S(1)} %get-tuple-element.21.end_other, ...), custom_call_target="tpu_custom_call" | custom-call | tf_op jit(solution)/shard_map/pallas_call | solution.py:33
  48.9 1.9 %collective-permute-start.3 = (f32[2,5,4,8,128]{4,3,2,1,0:T(8,128)S(1)}, f32[2,5,4,8,128]{4,3,2,1,0:T(8,128)S(1)}, u32[]{:S(2)}, u32[]{:S(2)}) collective-permute-start(f32[2,5,4,8,128]{4,3,2,1,0:T(8,128)S(1)} %get-tuple-element.23.end_other), channel_id=1, source_target_pairs={{0,16},{16,0},{32,48},{48,32},{64,80},{80,64},{96,112},{112,96},{1... | collective-permute-start | bytes 491528 | tf_op jit(solution)/shard_map/ppermute | solution.py:317
  50.8 8.1 %collective-permute-start.1 = (f32[2,5,4,8,128]{4,3,2,1,0:T(8,128)S(1)}, f32[2,5,4,8,128]{4,3,2,1,0:T(8,128)S(1)}, u32[]{:S(2)}, u32[]{:S(2)}) collective-permute-start(f32[2,5,4,8,128]{4,3,2,1,0:T(8,128)S(1)} %get-tuple-element.19.end_other), channel_id=1, source_target_pairs={{16,32},{32,16},{48,64},{64,48},{80,96},{96,80},{112,128},{128,112... | collective-permute-start | bytes 491528 | tf_op jit(solution)/shard_map/ppermute | solution.py:315
  58.9 0.0 collective-permute-done.3.entry
  58.9 1.9 %shard_map.90.refs_0_ = f32[4,2,2,4,8,128]{5,4,3,2,1,0:T(8,128)S(1)} custom-call(s32[3]{0:T(128)S(1)} %copy-done, f32[2,5,4,8,128]{4,3,2,1,0:T(8,128)S(1)} %collective-permute-done.3.entry, f32[2,5,4,8,128]{4,3,2,1,0:T(8,128)S(1)} %get-tuple-element.24.start_other, f32[2,5,4,8,128]{4,3,2,1,0:T(8,128)S(1)} %get-tuple-element.23.end_other, ...), custom_call_target="tpu_custom_call" | custom-call | tf_op jit(solution)/shard_map/pallas_call | solution.py:33
  60.8 3.4 %collective-permute-done.1.entry = f32[2,5,4,8,128]{4,3,2,1,0:T(8,128)S(1)} collective-permute-done((f32[2,5,4,8,128]{4,3,2,1,0:T(8,128)S(1)}, f32[2,5,4,8,128]{4,3,2,1,0:T(8,128)S(1)}, u32[]{:S(2)}, u32[]{:S(2)}) %collective-permute-start.1) | collective-permute-done | bytes 163872 | tf_op jit(solution)/shard_map/ppermute | solution.py:315
  64.2 1.9 %shard_map.91 = f32[4,4,2,4,8,128]{5,4,3,2,1,0:T(8,128)S(1)} custom-call(s32[3]{0:T(128)S(1)} %copy-done, f32[2,5,4,8,128]{4,3,2,1,0:T(8,128)S(1)} %collective-permute-done.1.entry, f32[2,5,4,8,128]{4,3,2,1,0:T(8,128)S(1)} %get-tuple-element.20.refs_0_.start_other, f32[2,5,4,8,128]{4,3,2,1,0:T(8,128)S(1)} %get-tuple-element.19.end_other, ...), custom_call_target="tpu_custom_call" | custom-call | tf_op jit(solution)/shard_map/pallas_call | solution.py:33
  66.1 19.3 %all_to_all.16.recv = f32[4,4,2,4,8,128]{5,4,3,2,1,0:T(8,128)S(1)} all-to-all(f32[4,4,2,4,8,128]{5,4,3,2,1,0:T(8,128)S(1)} %shard_map.91), channel_id=1, replica_groups=mesh['depth'=32,'strip'=4,'freq'=4] {'strip'}, dimensions={0} | all-to-all | bytes 1048576 | tf_op jit(solution)/shard_map/all_to_all | solution.py:320
  85.4 0.7 shard_map.93
  86.0 4.3 %all-to-all-start.2 = ((f32[4,2,2,2,8,128]{5,4,3,2,1,0:T(8,128)}), f32[4,2,2,2,8,128]{5,4,3,2,1,0:T(8,128)S(1)}, u32[]{:S(2)}, u32[]{:S(2)}) async-start(f32[4,2,2,2,8,128]{5,4,3,2,1,0:T(8,128)} %shard_map.93), calls=%async_computation.2 | async-start | bytes 262144 | tf_op jit(solution)/shard_map/all_to_all | solution.py:322
  90.3 0.8 shard_map.92
  91.1 5.2 %all-to-all-done.2.recv = f32[4,2,2,2,8,128]{5,4,3,2,1,0:T(8,128)S(1)} async-done(((f32[4,2,2,2,8,128]{5,4,3,2,1,0:T(8,128)}), f32[4,2,2,2,8,128]{5,4,3,2,1,0:T(8,128)S(1)}, u32[]{:S(2)}, u32[]{:S(2)}) %all-to-all-start.2) | async-done | bytes 131104 | tf_op jit(solution)/shard_map/all_to_all | solution.py:322
  96.3 0.6 shard_map.94
  (5 shorter events, 0.0 us)
Async XLA Ops:
  0.6 36.7 %copy-start.1 = (f32[64,2,2,8]{0,3,2,1:T(8,128)S(1)}, f32[64,2,2,8]{0,3,2,1:T(8,128)}, u32[]{:S(2)}) copy-start(f32[64,2,2,8]{0,3,2,1:T(8,128)} %param.11) | copy-start | bytes 24580
  1.3 30.0 %copy-start = (s32[3]{0:T(128)S(1)}, s32[3]{0:T(128)}, u32[]{:S(2)}) copy-start(s32[3]{0:T(128)} %pad_add_fusion.info) | copy-start | bytes 40
  32.1 7.8 %collective-permute-start = (f32[2,5,4,8,128]{4,3,2,1,0:T(8,128)S(1)}, f32[2,5,4,8,128]{4,3,2,1,0:T(8,128)S(1)}, u32[]{:S(2)}, u32[]{:S(2)}) collective-permute-start(f32[2,5,4,8,128]{4,3,2,1,0:T(8,128)S(1)} %get-tuple-element.15.end_other), channel_id=1, source_target_pairs={{0,16},{16,0},{32,48},{48,32},{64,80},{80,64},{96,112},{112,96},{1... | collective-permute-start | bytes 491528 | tf_op jit(solution)/shard_map/ppermute | solution.py:300
  34.1 12.9 %collective-permute-start.2 = (f32[2,5,4,8,128]{4,3,2,1,0:T(8,128)S(1)}, f32[2,5,4,8,128]{4,3,2,1,0:T(8,128)S(1)}, u32[]{:S(2)}, u32[]{:S(2)}) collective-permute-start(f32[2,5,4,8,128]{4,3,2,1,0:T(8,128)S(1)} %get-tuple-element.21.end_other), channel_id=1, source_target_pairs={{16,32},{32,16},{48,64},{64,48},{80,96},{96,80},{112,128},{128,112... | collective-permute-start | bytes 491528 | tf_op jit(solution)/shard_map/ppermute | solution.py:299
  48.9 10.0 %collective-permute-start.3 = (f32[2,5,4,8,128]{4,3,2,1,0:T(8,128)S(1)}, f32[2,5,4,8,128]{4,3,2,1,0:T(8,128)S(1)}, u32[]{:S(2)}, u32[]{:S(2)}) collective-permute-start(f32[2,5,4,8,128]{4,3,2,1,0:T(8,128)S(1)} %get-tuple-element.23.end_other), channel_id=1, source_target_pairs={{0,16},{16,0},{32,48},{48,32},{64,80},{80,64},{96,112},{112,96},{1... | collective-permute-start | bytes 491528 | tf_op jit(solution)/shard_map/ppermute | solution.py:317
  50.8 13.4 %collective-permute-start.1 = (f32[2,5,4,8,128]{4,3,2,1,0:T(8,128)S(1)}, f32[2,5,4,8,128]{4,3,2,1,0:T(8,128)S(1)}, u32[]{:S(2)}, u32[]{:S(2)}) collective-permute-start(f32[2,5,4,8,128]{4,3,2,1,0:T(8,128)S(1)} %get-tuple-element.19.end_other), channel_id=1, source_target_pairs={{16,32},{32,16},{48,64},{64,48},{80,96},{96,80},{112,128},{128,112... | collective-permute-start | bytes 491528 | tf_op jit(solution)/shard_map/ppermute | solution.py:315
  86.0 10.3 %all-to-all-start.2 = ((f32[4,2,2,2,8,128]{5,4,3,2,1,0:T(8,128)}), f32[4,2,2,2,8,128]{5,4,3,2,1,0:T(8,128)S(1)}, u32[]{:S(2)}, u32[]{:S(2)}) async-start(f32[4,2,2,2,8,128]{5,4,3,2,1,0:T(8,128)} %shard_map.93), calls=%async_computation.2 | async-start | bytes 262144 | tf_op jit(solution)/shard_map/all_to_all | solution.py:322

commit v3 on v2

--- a/solution.py
+++ b/solution.py
@@ -15,25 +15,23 @@
 WIDE = 5
 HALF = 4
 FOLD = 4
-VALUES = 12
 EDGE = 32
 PACK = LANES // EDGE
+FIRST = 4 * HALF + 1
 TILE = (ROWS, LANES)
 FIELD = (2, WIDE, FOLD) + TILE
 
 VM = pl.BlockSpec(memory_space=pltpu.VMEM)
-SM = pl.BlockSpec(memory_space=pltpu.SMEM)
 HB = pl.BlockSpec(memory_space=pltpu.HBM)
 
 
 def call(body, outs, scratch, limit, *args, stay=0):
     many = isinstance(outs, (list, tuple)) and isinstance(outs[0], (list, tuple))
     shapes = [jax.ShapeDtypeStruct(s, jnp.float32) for s in outs] if many else jax.ShapeDtypeStruct(outs, jnp.float32)
-    specs = [SM if n == 0 and a.dtype == jnp.int32 else HB if 1 <= n <= stay else VM for n, a in enumerate(args)]
     return pl.pallas_call(
         body,
         out_shape=shapes,
-        in_specs=specs,
+        in_specs=[HB if n < stay else VM for n in range(len(args))],
         out_specs=[VM] * len(outs) if many else VM,
         scratch_shapes=[pltpu.VMEM(s, jnp.float32) if isinstance(s, tuple) else s for s in scratch],
         compiler_params=pltpu.CompilerParams(vmem_limit_bytes=limit),
@@ -44,15 +42,15 @@
     return slice(tile * LANES, (tile + 1) * LANES)
 
 
-def pack_kernel(info, *refs):
-    _, _, _, _, _, send, fields, reflects, masks, cells, sems = refs
+def pack_kernel(*refs):
+    down, up, reflect, mask, classes, *turns, send2, fields, reflects, masks, cells, sems, send1 = refs
     held = (fields.at[0], fields.at[1], reflects, masks, cells)
     copies = [pltpu.make_async_copy(a, b, sems.at[n]) for n, (a, b) in enumerate(zip(refs[:5], held))]
     for copy in copies:
         copy.start()
     for copy in copies:
         copy.wait()
-    parity = info[0]
+    parity = lax.axis_index("depth") % 2
     lane = lax.broadcasted_iota(jnp.int32, TILE, 1)
     for tile in range(2 * HALF):
         at = columns(tile)
@@ -60,70 +58,66 @@
         shared += [cells[lv, :, at].astype(jnp.float32) for lv in range(2)]
         h = tile // HALF
         for f in range(2):
-            values = []
-            for r in (1 - parity, parity):
-                for level in (1 - r, r):
-                    values += [fields[r, level, p, f, :, at] for p in range(2)]
-            values += shared
-            for v, value in enumerate(values):
-                send[2 * h + f, HALF * v + tile % HALF] = value
-            if tile in (HALF - 1, HALF):
-                other = 1 - h
+            for r, more, send in ((1 - parity, [], send1), (parity, shared, send2)):
+                values = [fields[r, level, p, f, :, at] for level in (1 - r, r) for p in range(2)] + more
+                for v, value in enumerate(values):
+                    send[2 * h + f, HALF * v + tile % HALF] = value
+                if tile not in (HALF - 1, HALF):
+                    continue
                 from_lane = 0 if tile == HALF else LANES - EDGE
-                for group in range(VALUES // PACK):
+                for group in range(len(values) // PACK):
                     packed = None
                     for q in range(PACK):
                         shift = (EDGE * q - from_lane) % LANES
                         moved = values[PACK * group + q]
                         moved = pltpu.roll(moved, shift, 1) if shift else moved
                         packed = moved if packed is None else jnp.where(lane >= EDGE * q, moved, packed)
-                    send[2 * other + f, HALF * VALUES + group] = packed
-
-
-def fold_kernel(info, recv, first_end, first_start, second_end, second_start, coupling, cells, rows):
-    h = info[2]
+                    send[2 * (1 - h) + f, HALF * len(values) + group] = packed
+    here = lax.axis_index("strip")
+    for turn, out in enumerate(turns):
+        out[...] = send1[lax.rem(here + turn, FOLD)]
+
+
+def fold_kernel(sources, *refs):
+    recv, outs, rows = refs[:sources], refs[sources:-1], refs[-1]
+    values = 2 * len(outs)
+    here = lax.axis_index("strip")
+    h = here // 2
     lane = lax.broadcasted_iota(jnp.int32, TILE, 1)
     inside = jnp.where(h == 0, lane, LANES - 1 - lane) < EDGE
-    for s in range(FOLD):
-        at = slice(s * ROWS, (s + 1) * ROWS)
-        for v in range(VALUES):
+    for n in range(FOLD):
+        if sources == 1:
+            block, s = recv[0].at[n], n
+        else:
+            block, s = recv[n], lax.rem(here + FOLD - n, FOLD)
+        at = pl.ds(pl.multiple_of(s * ROWS, ROWS), ROWS)
+        for v in range(values):
             for j in range(HALF):
-                rows[v, h + j, at, :] = recv[s, HALF * v + j]
-            packed = recv[s, HALF * VALUES + v // PACK]
+                rows[v, h + j, at, :] = block[HALF * v + j]
+            packed = block[HALF * values + v // PACK]
             moved = pltpu.roll(packed, (LANES - EDGE * (v % PACK)) % LANES + (LANES - EDGE) * h, 1)
             rows[v, HALF * (1 - h), at, :] = jnp.where(inside, moved, 0.0)
-
-    def folded(v, j, i):
-        return rows[v, j, pl.ds(i, ROWS, stride=FOLD), :]
-
-    for j in range(WIDE):
-        for i in range(FOLD):
-            for p in range(2):
-                first_end[p, j, i] = folded(p, j, i)
-                first_start[p, j, i] = folded(2 + p, j, i)
-                second_end[p, j, i] = folded(4 + p, j, i)
-                second_start[p, j, i] = folded(6 + p, j, i)
-            for lv in range(2):
-                coupling[lv, j, i] = folded(8 + lv, j, i)
-                cells[lv, j, i] = folded(10 + lv, j, i)
-
-
-def table_kernel(info, cells, coeffs, table):
-    f = info[1]
-
-    def build(order, carry):
-        lookups = [jnp.broadcast_to(coeffs[f, p, pl.ds(order, 1), :], TILE) for p in range(2)]
+    for n, out in enumerate(outs):
+        for j in range(WIDE):
+            for i in range(FOLD):
+                for p in range(2):
+                    out[p, j, i] = rows[2 * n + p, j, pl.ds(i, ROWS, stride=FOLD), :]
+
+
+def table_kernel(cells, coeffs, table):
+    f = lax.axis_index("strip") % 2
+    spots = [(order, p) for order in range(TERMS) for p in range(2)]
+    lookups = [jnp.broadcast_to(coeffs[f, p, order : order + 1, :], TILE) for order, p in spots]
+
+    def build(j, carry):
         for lv in range(2):
-            for j in range(WIDE):
-                for i in range(FOLD):
-                    cls = cells[lv, j, i].astype(jnp.int32)
-                    for p in range(2):
-                        table[lv, order, p, j, i] = jnp.take_along_axis(
-                            lookups[p], cls, axis=1, mode="promise_in_bounds"
-                        )
+            for i in range(FOLD):
+                cls = cells[lv, j, i].astype(jnp.int32)
+                for (order, p), lookup in zip(spots, lookups):
+                    table[lv, order, p, j, i] = jnp.take_along_axis(lookup, cls, axis=1, mode="promise_in_bounds")
         return carry
 
-    lax.fori_loop(0, TERMS, build, 0)
+    lax.fori_loop(0, WIDE, build, 0)
 
 
 def filtered(read, write, level, table, terms, total):
@@ -180,13 +174,14 @@
                     write(1, j, i, imag)
 
 
-def direction(info, second):
-    return info[0] if second else 1 - info[0]
-
-
-def first_kernel(second, info, entry, start_other, end_other, coupling, table, *refs):
+def direction(second):
+    parity = lax.axis_index("depth") % 2
+    return parity if second else 1 - parity
+
+
+def first_kernel(second, entry, start_other, end_other, coupling, table, *refs):
     start_out, end_out, terms, total = refs[-4:]
-    r = direction(info, second)
+    r = direction(second)
     start, end = r, 1 - r
 
     def read_start(p, j, i):
@@ -205,12 +200,12 @@
     filtered(read_end, write_end, end, table, terms, total)
 
 
-def second_kernel(second, info, entry, start_other, end_other, coupling, table, *refs):
+def second_kernel(second, entry, start_other, end_other, coupling, table, *refs):
     if second:
         earlier, send, result, rows, terms, total = refs
     else:
         send, result, rows, terms, total = refs
-    r, h = direction(info, second), info[2]
+    r, h = direction(second), lax.axis_index("strip") // 2
     start, end = r, 1 - r
 
     def read_start(p, j, i):
@@ -269,6 +264,10 @@
                         out[lv, p, f, :, columns(tile)] = recv[2 * (tile // HALF) + f, 2 * n + lv, p, tile % HALF]
 
 
+def copy_kernel(source, target):
+    target[...] = source[...]
+
+
 def image_kernel(recv, image):
     for lv in range(2):
         for t in range(2):
@@ -279,37 +278,39 @@
 
 def local(down_state, up_state, reflect, layer_mask, classes, coeffs):
     depths = lax.axis_size("depth")
-    position = lax.axis_index("depth")
-    strip = lax.axis_index("strip")
-    info = jnp.stack([position % 2, strip % 2, strip // 2]).astype(jnp.int32)
     pairs = [(i, i ^ 1) for i in range(depths)]
     far = [q for i in range(1, depths - 1, 2) for q in ((i, i + 1), (i + 1, i))]
     lookup = jnp.pad(jnp.transpose(coeffs, (2, 1, 3, 0)), ((0, 0), (0, 0), (0, 0), (0, LANES - CLASSES)))
     sources = (down_state, up_state, reflect, layer_mask, classes)
     held = [pltpu.VMEM(a.shape, a.dtype) for a in (jax.ShapeDtypeStruct((2,) + up_state.shape, jnp.float32),) + sources[2:]]
-    send = call(
-        pack_kernel, (FOLD, HALF * VALUES + VALUES // PACK) + TILE,
-        held + [pltpu.SemaphoreType.DMA((5,))], 60 * 1024 * 1024, info, *sources, stay=5,
+    *turns, send2 = call(
+        pack_kernel, [(FIRST,) + TILE] * FOLD + [(FOLD, 2 * FIRST) + TILE],
+        held + [pltpu.SemaphoreType.DMA((5,)), (FOLD, FIRST) + TILE], 60 * 1024 * 1024, *sources, stay=5,
     )
-    recv = lax.all_to_all(send, "strip", 0, 0)
+    strips = range(lax.axis_size("strip"))
+    for turn in range(1, FOLD):
+        turns[turn] = lax.ppermute(turns[turn], "strip", [(s, (s + turn) % FOLD) for s in strips])
+    recv2 = lax.all_to_all(send2, "strip", 0, 0)
     folded = (2, WIDE, FOLD) + TILE
-    end1, start1, end2, start2, coupling, cells = call(
-        fold_kernel, [FIELD] * 4 + [folded] * 2, [(VALUES, WIDE, FOLD * ROWS, LANES)], 16 << 20, info, recv
+    rows = (WIDE, FOLD * ROWS, LANES)
+    end1, start1 = call(functools.partial(fold_kernel, 4), [FIELD] * 2, [(4,) + rows], 16 << 20, *turns)
+    from_far = lax.ppermute(end1, "depth", far)
+    lookup = call(copy_kernel, lookup.shape, [], 4 << 20, lookup)
+    end2, start2, coupling, cells = call(
+        functools.partial(fold_kernel, 1), [FIELD] * 2 + [folded] * 2, [(8,) + rows], 16 << 20, recv2
     )
-    from_far = lax.ppermute(end1, "depth", far)
     from_core = lax.ppermute(end2, "depth", pairs)
-    table = call(table_kernel, (2, TERMS) + FIELD, [], 16 << 20, info, cells, lookup)
+    table = call(table_kernel, (2, TERMS) + FIELD, [], 16 << 20, cells, lookup)
     work = [(3,) + FIELD, FIELD]
 
     def first(second, entry, other, *after):
         body = functools.partial(first_kernel, second)
-        return call(body, [FIELD, FIELD], work, 16 << 20, info, entry, *other, coupling, table, *after)
+        return call(body, [FIELD, FIELD], work, 16 << 20, entry, *other, coupling, table, *after)
 
     def last(second, entry, other, *earlier):
         body = functools.partial(second_kernel, second)
         out = (FOLD, 4 if second else 2, 2, HALF) + TILE
-        scratch = [FIELD, (2, WIDE, FOLD * ROWS, LANES)] + work
-        return call(body, out, scratch, 16 << 20, info, entry, *other, coupling, table, *earlier)
+        return call(body, out, [FIELD, (2,) + rows] + work, 16 << 20, entry, *other, coupling, table, *earlier)
 
     one = first(False, from_core, (start2, end2))
     ahead = lax.ppermute(one[1], "depth", far)

time: 97.3 us -> 93.3 us (0.959)
  blocking collectives: 46.3 us -> 19.7 us
  starting transfers between devices: 19.4 us -> 35.6 us
  waiting for transfers between devices: 13.7 us -> 24.5 us
  Pallas kernels: 16 us -> 11.1 us
    all_to_all x2 -> x1, blocking collectives: 46.3 us -> 19.7 us  [local(): recv = lax.all_to_all(send, 'strip', 0, 0)]
    ppermute x0 -> x3, starting transfers between devices: none -> 11.6 us  [local(): lax.ppermute(turns[turn], 'strip', [(s, (s + turn) % FOLD) for s in strips])]
    all_to_all x0 -> x1, waiting for transfers between devices: none -> 7.59 us  [local(): recv2 = lax.all_to_all(send2, 'strip', 0, 0)]
    all_to_all x0 -> x1, starting transfers between devices: none -> 5.91 us  [local(): recv2 = lax.all_to_all(send2, 'strip', 0, 0)]
    pallas_call x10 -> x12, Pallas kernels: 16 us -> 11.1 us  [call(): pl.pallas_call(body, out_shape=shapes, in_specs=[HB if n < stay else VM f...]
    ppermute x1, waiting for transfers between devices: 5.14 us -> 7.13 us  [local(): from_far = lax.ppermute(end1, 'depth', far)]
    ppermute x1, waiting for transfers between devices: 3.36 us -> 4.65 us  [local(): ahead = lax.ppermute(one[1], 'depth', far)]
    ppermute x1, starting transfers between devices: 8.08 us -> 6.82 us  [local(): ahead = lax.ppermute(one[1], 'depth', far)]
  transfers between devices with their start and end apart: 5 -> 9, of which waited for: 3 -> 4; matrix products, arithmetic and copies ran while one was open for 0% -> 0% of each run, Pallas kernels for 7% -> 5%
where the time goes in v3:
time: 93.3 us; the launch traced here: 92.7 us
  starting transfers between devices  35.6 us (38%)
  waiting for transfers between devices  24.5 us (26%)
  blocking collectives  19.7 us (21%)
  Pallas kernels  11.1 us (12%)
    all_to_all x1, blocking collectives, local(): recv = lax.all_to_all(send, 'strip', 0, 0)  19.7 us
    ppermute x3, starting transfers between devices, local(): lax.ppermute(turns[turn], 'strip', [(s, (s + turn) % FOLD) for s in strips])  11.6 us
    pallas_call x12, Pallas kernels, call(): pl.pallas_call(body, out_shape=shapes, in_specs=[HB if n < stay else VM f...  11.1 us
    all_to_all x1, waiting for transfers between devices, local(): recv2 = lax.all_to_all(send2, 'strip', 0, 0)  7.59 us
    ppermute x1, waiting for transfers between devices, local(): from_far = lax.ppermute(end1, 'depth', far)  7.13 us
    ppermute x1, starting transfers between devices, local(): ahead = lax.ppermute(one[1], 'depth', far)  6.82 us
    all_to_all x1, starting transfers between devices, local(): recv2 = lax.all_to_all(send2, 'strip', 0, 0)  5.91 us
    all_to_all x1, waiting for transfers between devices, local(): sums = lax.all_to_all(sums, 'freq', 0, 0)  5.15 us
  transfers between devices with their start and end apart: 9, of which 4 were waited for; matrix products, arithmetic and copies ran while one was open for 0% of the time, Pallas kernels for 5%

profile of v3, /device:TPU:128, one launch (start us, length us, event | category | flops | bytes accessed | tf_op | source)
XLA Modules:
  0.0 92.7 jit_solution(17080765570408886960)
XLA Ops:
  0.6 2.1 %shard_map.85 = (f32[17,8,128]{2,1,0:T(8,128)}, f32[17,8,128]{2,1,0:T(8,128)}, f32[17,8,128]{2,1,0:T(8,128)}, f32[17,8,128]{2,1,0:T(8,128)}, f32[4,34,8,128]{3,2,1,0:T(8,128)}) custom-call(f32[2,2,2,8,1024]{4,3,2,1,0:T(8,128)} %refs_0_.1, f32[2,2,2,8,1024]{4,3,2,1,0:T(8,128)} %refs_1_.1, f32[2,8,1024]{2,1,0:T(8,128)} %refs_2_.1, s32[2,8,1024]{2,1,0:T(8,128)} %refs_3_.1, ...), custom_call_target="tpu_custom_call" | custom-call | tf_op jit(solution)/shard_map/pallas_call | solution.py:31
  2.7 5.9 %all-to-all-start = ((f32[4,34,8,128]{3,2,1,0:T(8,128)}), f32[4,34,8,128]{3,2,1,0:T(8,128)S(1)}, u32[]{:S(2)}, u32[]{:S(2)}) async-start(f32[4,34,8,128]{3,2,1,0:T(8,128)} %get-tuple-element.20), calls=%async_computation | async-start | bytes 1114112 | tf_op jit(solution)/shard_map/all_to_all | solution.py:293
  8.6 3.9 %collective-permute-start.2 = (f32[17,8,128]{2,1,0:T(8,128)}, f32[17,8,128]{2,1,0:T(8,128)S(1)}, u32[]{:S(2)}, u32[]{:S(2)}) collective-permute-start(f32[17,8,128]{2,1,0:T(8,128)} %get-tuple-element.28), channel_id=1, source_target_pairs={{0,4},{4,8},{8,12},{12,0},{1,5},{5,9},{9,13},{13,1},{2,6},{6,10},{... | collective-permute-start | bytes 208904 | tf_op jit(solution)/shard_map/ppermute | solution.py:292
  12.6 4.3 %collective-permute-start.3 = (f32[17,8,128]{2,1,0:T(8,128)}, f32[17,8,128]{2,1,0:T(8,128)S(1)}, u32[]{:S(2)}, u32[]{:S(2)}) collective-permute-start(f32[17,8,128]{2,1,0:T(8,128)} %get-tuple-element.29), channel_id=1, source_target_pairs={{0,8},{4,12},{8,0},{12,4},{1,9},{5,13},{9,1},{13,5},{2,10},{6,14},... | collective-permute-start | bytes 208904 | tf_op jit(solution)/shard_map/ppermute | solution.py:292
  16.9 3.4 %collective-permute-start.4 = (f32[17,8,128]{2,1,0:T(8,128)}, f32[17,8,128]{2,1,0:T(8,128)S(1)}, u32[]{:S(2)}, u32[]{:S(2)}) collective-permute-start(f32[17,8,128]{2,1,0:T(8,128)} %get-tuple-element.30), channel_id=1, source_target_pairs={{0,12},{4,0},{8,4},{12,8},{1,13},{5,1},{9,5},{13,9},{2,14},{6,2},{... | collective-permute-start | bytes 208904 | tf_op jit(solution)/shard_map/ppermute | solution.py:292
  20.2 7.6 %all-to-all-done.refs_0_ = f32[4,34,8,128]{3,2,1,0:T(8,128)S(1)} async-done(((f32[4,34,8,128]{3,2,1,0:T(8,128)}), f32[4,34,8,128]{3,2,1,0:T(8,128)S(1)}, u32[]{:S(2)}, u32[]{:S(2)}) %all-to-all-start) | async-done | bytes 557088 | tf_op jit(solution)/shard_map/all_to_all | solution.py:293
  28.0 1.9 %collective-permute-start = (f32[2,5,4,8,128]{4,3,2,1,0:T(8,128)S(1)}, f32[2,5,4,8,128]{4,3,2,1,0:T(8,128)S(1)}, u32[]{:S(2)}, u32[]{:S(2)}) collective-permute-start(f32[2,5,4,8,128]{4,3,2,1,0:T(8,128)S(1)} %get-tuple-element.21.end_other), channel_id=1, source_target_pairs={{0,16},{16,0},{32,48},{48,32},{64,80},{80,64},{96,112},{112,96},{1... | collective-permute-start | bytes 491528 | tf_op jit(solution)/shard_map/ppermute | solution.py:302
  30.0 0.9 copy-done
  31.0 3.2 %collective-permute-start.5 = (f32[2,5,4,8,128]{4,3,2,1,0:T(8,128)S(1)}, f32[2,5,4,8,128]{4,3,2,1,0:T(8,128)S(1)}, u32[]{:S(2)}, u32[]{:S(2)}) collective-permute-start(f32[2,5,4,8,128]{4,3,2,1,0:T(8,128)S(1)} %get-tuple-element.31.end_other), channel_id=1, source_target_pairs={{16,32},{32,16},{48,64},{64,48},{80,96},{96,80},{112,128},{128,112... | collective-permute-start | bytes 491528 | tf_op jit(solution)/shard_map/ppermute | solution.py:297
  34.3 1.1 %shard_map.88.table = f32[2,8,2,5,4,8,128]{6,5,4,3,2,1,0:T(8,128)S(1)} custom-call(f32[2,5,4,8,128]{4,3,2,1,0:T(8,128)S(1)} %get-tuple-element.24.cells, f32[2,2,8,128]{3,2,1,0:T(8,128)S(1)} %shard_map.87.coeffs), custom_call_target="tpu_custom_call" | custom-call | tf_op jit(solution)/shard_map/pallas_call | solution.py:31
  35.5 1.3 %shard_map.89 = (f32[2,5,4,8,128]{4,3,2,1,0:T(8,128)S(1)}, f32[2,5,4,8,128]{4,3,2,1,0:T(8,128)S(1)}) custom-call(f32[2,5,4,8,128]{4,3,2,1,0:T(8,128)S(1)} %collective-permute-done.entry, f32[2,5,4,8,128]{4,3,2,1,0:T(8,128)S(1)} %get-tuple-element.22.start_other, f32[2,5,4,8,128]{4,3,2,1,0:T(8,128)S(1)} %get-tuple-element.21.end_other, ...), custom_call_target="tpu_custom_call" | custom-call | tf_op jit(solution)/shard_map/pallas_call | solution.py:31
  36.8 7.1 %collective-permute-done.5.entry = f32[2,5,4,8,128]{4,3,2,1,0:T(8,128)S(1)} collective-permute-done((f32[2,5,4,8,128]{4,3,2,1,0:T(8,128)S(1)}, f32[2,5,4,8,128]{4,3,2,1,0:T(8,128)S(1)}, u32[]{:S(2)}, u32[]{:S(2)}) %collective-permute-start.5) | collective-permute-done | bytes 163872 | tf_op jit(solution)/shard_map/ppermute | solution.py:297
  43.9 1.3 %shard_map.91 = (f32[2,5,4,8,128]{4,3,2,1,0:T(8,128)S(1)}, f32[2,5,4,8,128]{4,3,2,1,0:T(8,128)S(1)}) custom-call(f32[2,5,4,8,128]{4,3,2,1,0:T(8,128)S(1)} %collective-permute-done.5.entry, f32[2,5,4,8,128]{4,3,2,1,0:T(8,128)S(1)} %get-tuple-element.32.start_other, f32[2,5,4,8,128]{4,3,2,1,0:T(8,128)S(1)} %get-tuple-element.31.end_other, ...), custom_call_target="tpu_custom_call" | custom-call | tf_op jit(solution)/shard_map/pallas_call | solution.py:31
  45.3 1.9 %collective-permute-start.6 = (f32[2,5,4,8,128]{4,3,2,1,0:T(8,128)S(1)}, f32[2,5,4,8,128]{4,3,2,1,0:T(8,128)S(1)}, u32[]{:S(2)}, u32[]{:S(2)}) collective-permute-start(f32[2,5,4,8,128]{4,3,2,1,0:T(8,128)S(1)} %get-tuple-element.33.end_other), channel_id=1, source_target_pairs={{0,16},{16,0},{32,48},{48,32},{64,80},{80,64},{96,112},{112,96},{1... | collective-permute-start | bytes 491528 | tf_op jit(solution)/shard_map/ppermute | solution.py:318
  47.2 6.8 %collective-permute-start.1 = (f32[2,5,4,8,128]{4,3,2,1,0:T(8,128)S(1)}, f32[2,5,4,8,128]{4,3,2,1,0:T(8,128)S(1)}, u32[]{:S(2)}, u32[]{:S(2)}) collective-permute-start(f32[2,5,4,8,128]{4,3,2,1,0:T(8,128)S(1)} %get-tuple-element.25.end_other), channel_id=1, source_target_pairs={{16,32},{32,16},{48,64},{64,48},{80,96},{96,80},{112,128},{128,112... | collective-permute-start | bytes 491528 | tf_op jit(solution)/shard_map/ppermute | solution.py:316
  54.0 1.4 %shard_map.92.refs_0_ = f32[4,2,2,4,8,128]{5,4,3,2,1,0:T(8,128)S(1)} custom-call(f32[2,5,4,8,128]{4,3,2,1,0:T(8,128)S(1)} %collective-permute-done.6.entry, f32[2,5,4,8,128]{4,3,2,1,0:T(8,128)S(1)} %get-tuple-element.34.start_other, f32[2,5,4,8,128]{4,3,2,1,0:T(8,128)S(1)} %get-tuple-element.33.end_other, ...), custom_call_target="tpu_custom_call" | custom-call | tf_op jit(solution)/shard_map/pallas_call | solution.py:31
  55.4 4.7 %collective-permute-done.1.entry = f32[2,5,4,8,128]{4,3,2,1,0:T(8,128)S(1)} collective-permute-done((f32[2,5,4,8,128]{4,3,2,1,0:T(8,128)S(1)}, f32[2,5,4,8,128]{4,3,2,1,0:T(8,128)S(1)}, u32[]{:S(2)}, u32[]{:S(2)}) %collective-permute-start.1) | collective-permute-done | bytes 163872 | tf_op jit(solution)/shard_map/ppermute | solution.py:316
  60.1 1.4 %shard_map.93 = f32[4,4,2,4,8,128]{5,4,3,2,1,0:T(8,128)S(1)} custom-call(f32[2,5,4,8,128]{4,3,2,1,0:T(8,128)S(1)} %collective-permute-done.1.entry, f32[2,5,4,8,128]{4,3,2,1,0:T(8,128)S(1)} %get-tuple-element.26.refs_0_.start_other, f32[2,5,4,8,128]{4,3,2,1,0:T(8,128)S(1)} %get-tuple-element.25.end_other, ...), custom_call_target="tpu_custom_call" | custom-call | tf_op jit(solution)/shard_map/pallas_call | solution.py:31
  61.4 19.7 %all_to_all.15.recv = f32[4,4,2,4,8,128]{5,4,3,2,1,0:T(8,128)S(1)} all-to-all(f32[4,4,2,4,8,128]{5,4,3,2,1,0:T(8,128)S(1)} %shard_map.93), channel_id=1, replica_groups=mesh['depth'=32,'strip'=4,'freq'=4] {'strip'}, dimensions={0} | all-to-all | bytes 1048576 | tf_op jit(solution)/shard_map/all_to_all | solution.py:321
  81.1 0.7 shard_map.95
  81.8 4.3 %all-to-all-start.2 = ((f32[4,2,2,2,8,128]{5,4,3,2,1,0:T(8,128)}), f32[4,2,2,2,8,128]{5,4,3,2,1,0:T(8,128)S(1)}, u32[]{:S(2)}, u32[]{:S(2)}) async-start(f32[4,2,2,2,8,128]{5,4,3,2,1,0:T(8,128)} %shard_map.95), calls=%async_computation.2 | async-start | bytes 262144 | tf_op jit(solution)/shard_map/all_to_all | solution.py:323
  86.1 0.8 shard_map.94
  86.9 5.2 %all-to-all-done.2.recv = f32[4,2,2,2,8,128]{5,4,3,2,1,0:T(8,128)S(1)} async-done(((f32[4,2,2,2,8,128]{5,4,3,2,1,0:T(8,128)}), f32[4,2,2,2,8,128]{5,4,3,2,1,0:T(8,128)S(1)}, u32[]{:S(2)}, u32[]{:S(2)}) %all-to-all-start.2) | async-done | bytes 131104 | tf_op jit(solution)/shard_map/all_to_all | solution.py:323
  92.1 0.6 shard_map.96
  (13 shorter events, 0.4 us)
Async XLA Ops:
  0.6 33.6 %copy-start.1 = (f32[64,2,2,8]{0,3,2,1:T(8,128)S(1)}, f32[64,2,2,8]{0,3,2,1:T(8,128)}, u32[]{:S(2)}) copy-start(f32[64,2,2,8]{0,3,2,1:T(8,128)} %param.11) | copy-start | bytes 24580
  2.7 25.1 %all-to-all-start = ((f32[4,34,8,128]{3,2,1,0:T(8,128)}), f32[4,34,8,128]{3,2,1,0:T(8,128)S(1)}, u32[]{:S(2)}, u32[]{:S(2)}) async-start(f32[4,34,8,128]{3,2,1,0:T(8,128)} %get-tuple-element.20), calls=%async_computation | async-start | bytes 1114112 | tf_op jit(solution)/shard_map/all_to_all | solution.py:293
  8.6 21.3 %collective-permute-start.2 = (f32[17,8,128]{2,1,0:T(8,128)}, f32[17,8,128]{2,1,0:T(8,128)S(1)}, u32[]{:S(2)}, u32[]{:S(2)}) collective-permute-start(f32[17,8,128]{2,1,0:T(8,128)} %get-tuple-element.28), channel_id=1, source_target_pairs={{0,4},{4,8},{8,12},{12,0},{1,5},{5,9},{9,13},{13,1},{2,6},{6,10},{... | collective-permute-start | bytes 208904 | tf_op jit(solution)/shard_map/ppermute | solution.py:292
  12.6 17.4 %collective-permute-start.3 = (f32[17,8,128]{2,1,0:T(8,128)}, f32[17,8,128]{2,1,0:T(8,128)S(1)}, u32[]{:S(2)}, u32[]{:S(2)}) collective-permute-start(f32[17,8,128]{2,1,0:T(8,128)} %get-tuple-element.29), channel_id=1, source_target_pairs={{0,8},{4,12},{8,0},{12,4},{1,9},{5,13},{9,1},{13,5},{2,10},{6,14},... | collective-permute-start | bytes 208904 | tf_op jit(solution)/shard_map/ppermute | solution.py:292
  16.9 13.1 %collective-permute-start.4 = (f32[17,8,128]{2,1,0:T(8,128)}, f32[17,8,128]{2,1,0:T(8,128)S(1)}, u32[]{:S(2)}, u32[]{:S(2)}) collective-permute-start(f32[17,8,128]{2,1,0:T(8,128)} %get-tuple-element.30), channel_id=1, source_target_pairs={{0,12},{4,0},{8,4},{12,8},{1,13},{5,1},{9,5},{13,9},{2,14},{6,2},{... | collective-permute-start | bytes 208904 | tf_op jit(solution)/shard_map/ppermute | solution.py:292
  28.0 7.4 %collective-permute-start = (f32[2,5,4,8,128]{4,3,2,1,0:T(8,128)S(1)}, f32[2,5,4,8,128]{4,3,2,1,0:T(8,128)S(1)}, u32[]{:S(2)}, u32[]{:S(2)}) collective-permute-start(f32[2,5,4,8,128]{4,3,2,1,0:T(8,128)S(1)} %get-tuple-element.21.end_other), channel_id=1, source_target_pairs={{0,16},{16,0},{32,48},{48,32},{64,80},{80,64},{96,112},{112,96},{1... | collective-permute-start | bytes 491528 | tf_op jit(solution)/shard_map/ppermute | solution.py:302
  30.0 0.9 copy-start
  31.0 12.9 %collective-permute-start.5 = (f32[2,5,4,8,128]{4,3,2,1,0:T(8,128)S(1)}, f32[2,5,4,8,128]{4,3,2,1,0:T(8,128)S(1)}, u32[]{:S(2)}, u32[]{:S(2)}) collective-permute-start(f32[2,5,4,8,128]{4,3,2,1,0:T(8,128)S(1)} %get-tuple-element.31.end_other), channel_id=1, source_target_pairs={{16,32},{32,16},{48,64},{64,48},{80,96},{96,80},{112,128},{128,112... | collective-permute-start | bytes 491528 | tf_op jit(solution)/shard_map/ppermute | solution.py:297
  45.3 8.8 %collective-permute-start.6 = (f32[2,5,4,8,128]{4,3,2,1,0:T(8,128)S(1)}, f32[2,5,4,8,128]{4,3,2,1,0:T(8,128)S(1)}, u32[]{:S(2)}, u32[]{:S(2)}) collective-permute-start(f32[2,5,4,8,128]{4,3,2,1,0:T(8,128)S(1)} %get-tuple-element.33.end_other), channel_id=1, source_target_pairs={{0,16},{16,0},{32,48},{48,32},{64,80},{80,64},{96,112},{112,96},{1... | collective-permute-start | bytes 491528 | tf_op jit(solution)/shard_map/ppermute | solution.py:318
  47.2 12.9 %collective-permute-start.1 = (f32[2,5,4,8,128]{4,3,2,1,0:T(8,128)S(1)}, f32[2,5,4,8,128]{4,3,2,1,0:T(8,128)S(1)}, u32[]{:S(2)}, u32[]{:S(2)}) collective-permute-start(f32[2,5,4,8,128]{4,3,2,1,0:T(8,128)S(1)} %get-tuple-element.25.end_other), channel_id=1, source_target_pairs={{16,32},{32,16},{48,64},{64,48},{80,96},{96,80},{112,128},{128,112... | collective-permute-start | bytes 491528 | tf_op jit(solution)/shard_map/ppermute | solution.py:316
  81.8 10.3 %all-to-all-start.2 = ((f32[4,2,2,2,8,128]{5,4,3,2,1,0:T(8,128)}), f32[4,2,2,2,8,128]{5,4,3,2,1,0:T(8,128)S(1)}, u32[]{:S(2)}, u32[]{:S(2)}) async-start(f32[4,2,2,2,8,128]{5,4,3,2,1,0:T(8,128)} %shard_map.95), calls=%async_computation.2 | async-start | bytes 262144 | tf_op jit(solution)/shard_map/all_to_all | solution.py:323

commit v4 on v3

--- a/solution.py
+++ b/solution.py
@@ -20,6 +20,7 @@
 FIRST = 4 * HALF + 1
 TILE = (ROWS, LANES)
 FIELD = (2, WIDE, FOLD) + TILE
+MESSAGE = (2 * HALF * FOLD + 2,) + TILE
 
 VM = pl.BlockSpec(memory_space=pltpu.VMEM)
 HB = pl.BlockSpec(memory_space=pltpu.HBM)
@@ -78,13 +79,42 @@
         out[...] = send1[lax.rem(here + turn, FOLD)]
 
 
+def halo_of(packed, q, h):
+    lane = lax.broadcasted_iota(jnp.int32, TILE, 1)
+    inside = jnp.where(h == 0, lane, LANES - 1 - lane) < EDGE
+    moved = pltpu.roll(packed, (LANES - EDGE * q) % LANES + (LANES - EDGE) * h, 1)
+    return jnp.where(inside, moved, 0.0)
+
+
+def put_message(message, field):
+    h = lax.axis_index("strip") // 2
+    lane = lax.broadcasted_iota(jnp.int32, TILE, 1)
+    for p in range(2):
+        packed = None
+        for i in range(FOLD):
+            for j in range(HALF):
+                message[(p * HALF + j) * FOLD + i] = field[p, h + j, i]
+            moved = pltpu.roll(field[p, HALF * (1 - h), i], EDGE * (i + h), 1)
+            packed = moved if packed is None else jnp.where(lane >= EDGE * i, moved, packed)
+        message[2 * HALF * FOLD + p] = packed
+
+
+def take_message(message, field):
+    h = lax.axis_index("strip") // 2
+    for p in range(2):
+        for i in range(FOLD):
+            for j in range(HALF):
+                field[p, h + j, i] = message[(p * HALF + j) * FOLD + i]
+            field[p, HALF * (1 - h), i] = halo_of(message[2 * HALF * FOLD + p], i, h)
+
+
 def fold_kernel(sources, *refs):
     recv, outs, rows = refs[:sources], refs[sources:-1], refs[-1]
+    if sources > 1:
+        outs, message = outs[:-1], outs[-1]
     values = 2 * len(outs)
     here = lax.axis_index("strip")
     h = here // 2
-    lane = lax.broadcasted_iota(jnp.int32, TILE, 1)
-    inside = jnp.where(h == 0, lane, LANES - 1 - lane) < EDGE
     for n in range(FOLD):
         if sources == 1:
             block, s = recv[0].at[n], n
@@ -94,14 +124,14 @@
         for v in range(values):
             for j in range(HALF):
                 rows[v, h + j, at, :] = block[HALF * v + j]
-            packed = block[HALF * values + v // PACK]
-            moved = pltpu.roll(packed, (LANES - EDGE * (v % PACK)) % LANES + (LANES - EDGE) * h, 1)
-            rows[v, HALF * (1 - h), at, :] = jnp.where(inside, moved, 0.0)
+            rows[v, HALF * (1 - h), at, :] = halo_of(block[HALF * values + v // PACK], v % PACK, h)
     for n, out in enumerate(outs):
         for j in range(WIDE):
             for i in range(FOLD):
                 for p in range(2):
                     out[p, j, i] = rows[2 * n + p, j, pl.ds(i, ROWS, stride=FOLD), :]
+    if sources > 1:
+        put_message(message, outs[0])
 
 
 def table_kernel(cells, coeffs, table):
@@ -180,7 +210,12 @@
 
 
 def first_kernel(second, entry, start_other, end_other, coupling, table, *refs):
-    start_out, end_out, terms, total = refs[-4:]
+    if second:
+        start_out, end_out, field, terms, total = refs[-5:]
+        take_message(entry, field)
+        entry = field
+    else:
+        start_out, end_out, message, terms, total = refs[-5:]
     r = direction(second)
     start, end = r, 1 - r
 
@@ -198,11 +233,15 @@
 
     filtered(read_start, write_start, start, table, terms, total)
     filtered(read_end, write_end, end, table, terms, total)
+    if not second:
+        put_message(message, end_out)
 
 
 def second_kernel(second, entry, start_other, end_other, coupling, table, *refs):
     if second:
-        earlier, send, result, rows, terms, total = refs
+        earlier, send, field, result, rows, terms, total = refs
+        take_message(entry, field)
+        entry = field
     else:
         send, result, rows, terms, total = refs
     r, h = direction(second), lax.axis_index("strip") // 2
@@ -293,8 +332,10 @@
     recv2 = lax.all_to_all(send2, "strip", 0, 0)
     folded = (2, WIDE, FOLD) + TILE
     rows = (WIDE, FOLD * ROWS, LANES)
-    end1, start1 = call(functools.partial(fold_kernel, 4), [FIELD] * 2, [(4,) + rows], 16 << 20, *turns)
-    from_far = lax.ppermute(end1, "depth", far)
+    end1, start1, message = call(
+        functools.partial(fold_kernel, 4), [FIELD] * 2 + [MESSAGE], [(4,) + rows], 16 << 20, *turns
+    )
+    from_far = lax.ppermute(message, "depth", far)
     lookup = call(copy_kernel, lookup.shape, [], 4 << 20, lookup)
     end2, start2, coupling, cells = call(
         functools.partial(fold_kernel, 1), [FIELD] * 2 + [folded] * 2, [(8,) + rows], 16 << 20, recv2
@@ -305,19 +346,21 @@
 
     def first(second, entry, other, *after):
         body = functools.partial(first_kernel, second)
-        return call(body, [FIELD, FIELD], work, 16 << 20, entry, *other, coupling, table, *after)
+        outs, scratch = ([FIELD] * 2, [FIELD] + work) if second else ([FIELD] * 2 + [MESSAGE], work)
+        return call(body, outs, scratch, 16 << 20, entry, *other, coupling, table, *after)
 
     def last(second, entry, other, *earlier):
         body = functools.partial(second_kernel, second)
         out = (FOLD, 4 if second else 2, 2, HALF) + TILE
-        return call(body, out, [FIELD, (2,) + rows] + work, 16 << 20, entry, *other, coupling, table, *earlier)
+        scratch = [FIELD] * (2 if second else 1) + [(2,) + rows] + work
+        return call(body, out, scratch, 16 << 20, entry, *other, coupling, table, *earlier)
 
     one = first(False, from_core, (start2, end2))
-    ahead = lax.ppermute(one[1], "depth", far)
+    ahead = lax.ppermute(one[2], "depth", far)
     two = first(True, from_far, (start1, end1), one[0])
     from_core = lax.ppermute(two[1], "depth", pairs)
     part = last(False, from_core, two)
-    send = last(True, ahead, one, part)
+    send = last(True, ahead, one[:2], part)
     recv = lax.all_to_all(send, "strip", 0, 0)
     sums = call(sums_kernel, (4, 2, 2, 2) + TILE, [], 16 << 20, recv)
     sums = lax.all_to_all(sums, "freq", 0, 0)

time: 93.3 us -> 90.6 us (0.971)
  blocking collectives: 19.7 us -> 17.6 us
    all_to_all x1, blocking collectives: 19.7 us -> 17.6 us  [local(): recv = lax.all_to_all(send, 'strip', 0, 0)]
  transfers between devices with their start and end apart: 9 -> 9, of which waited for: 4 -> 4; matrix products, arithmetic and copies ran while one was open for 0% -> 0% of each run, Pallas kernels for 5% -> 6%
where the time goes in v4:
time: 90.6 us; the launch traced here: 90.1 us
  starting transfers between devices  35 us (39%)
  waiting for transfers between devices  24.3 us (27%)
  blocking collectives  17.6 us (19%)
  Pallas kernels  11.5 us (13%)
    all_to_all x1, blocking collectives, local(): recv = lax.all_to_all(send, 'strip', 0, 0)  17.6 us
    ppermute x3, starting transfers between devices, local(): lax.ppermute(turns[turn], 'strip', [(s, (s + turn) % FOLD) for s in strips])  11.6 us
    pallas_call x12, Pallas kernels, call(): pl.pallas_call(body, out_shape=shapes, in_specs=[HB if n < stay else VM f...  11.5 us
    all_to_all x1, waiting for transfers between devices, local(): recv2 = lax.all_to_all(send2, 'strip', 0, 0)  7.59 us
    ppermute x1, waiting for transfers between devices, local(): from_far = lax.ppermute(message, 'depth', far)  6.65 us
    ppermute x1, starting transfers between devices, local(): ahead = lax.ppermute(one[2], 'depth', far)  6.18 us
    all_to_all x1, starting transfers between devices, local(): recv2 = lax.all_to_all(send2, 'strip', 0, 0)  5.91 us
    all_to_all x1, waiting for transfers between devices, local(): sums = lax.all_to_all(sums, 'freq', 0, 0)  5.15 us
  transfers between devices with their start and end apart: 9, of which 4 were waited for; matrix products, arithmetic and copies ran while one was open for 0% of the time, Pallas kernels for 6%

profile of v4, /device:TPU:128, one launch (start us, length us, event | category | flops | bytes accessed | tf_op | source)
XLA Modules:
  0.0 90.1 jit_solution(10738809327240857105)
XLA Ops:
  0.6 2.1 %shard_map.85 = (f32[17,8,128]{2,1,0:T(8,128)}, f32[17,8,128]{2,1,0:T(8,128)}, f32[17,8,128]{2,1,0:T(8,128)}, f32[17,8,128]{2,1,0:T(8,128)}, f32[4,34,8,128]{3,2,1,0:T(8,128)}) custom-call(f32[2,2,2,8,1024]{4,3,2,1,0:T(8,128)} %refs_0_.1, f32[2,2,2,8,1024]{4,3,2,1,0:T(8,128)} %refs_1_.1, f32[2,8,1024]{2,1,0:T(8,128)} %refs_2_.1, s32[2,8,1024]{2,1,0:T(8,128)} %refs_3_.1, ...), custom_call_target="tpu_custom_call" | custom-call | tf_op jit(solution)/shard_map/pallas_call | solution.py:32
  2.7 5.9 %all-to-all-start = ((f32[4,34,8,128]{3,2,1,0:T(8,128)}), f32[4,34,8,128]{3,2,1,0:T(8,128)S(1)}, u32[]{:S(2)}, u32[]{:S(2)}) async-start(f32[4,34,8,128]{3,2,1,0:T(8,128)} %get-tuple-element.22), calls=%async_computation | async-start | bytes 1114112 | tf_op jit(solution)/shard_map/all_to_all | solution.py:332
  8.6 3.9 %collective-permute-start.2 = (f32[17,8,128]{2,1,0:T(8,128)}, f32[17,8,128]{2,1,0:T(8,128)S(1)}, u32[]{:S(2)}, u32[]{:S(2)}) collective-permute-start(f32[17,8,128]{2,1,0:T(8,128)} %get-tuple-element.31), channel_id=1, source_target_pairs={{0,4},{4,8},{8,12},{12,0},{1,5},{5,9},{9,13},{13,1},{2,6},{6,10},{... | collective-permute-start | bytes 208904 | tf_op jit(solution)/shard_map/ppermute | solution.py:331
  12.6 4.3 %collective-permute-start.3 = (f32[17,8,128]{2,1,0:T(8,128)}, f32[17,8,128]{2,1,0:T(8,128)S(1)}, u32[]{:S(2)}, u32[]{:S(2)}) collective-permute-start(f32[17,8,128]{2,1,0:T(8,128)} %get-tuple-element.32), channel_id=1, source_target_pairs={{0,8},{4,12},{8,0},{12,4},{1,9},{5,13},{9,1},{13,5},{2,10},{6,14},... | collective-permute-start | bytes 208904 | tf_op jit(solution)/shard_map/ppermute | solution.py:331
  16.9 3.4 %collective-permute-start.4 = (f32[17,8,128]{2,1,0:T(8,128)}, f32[17,8,128]{2,1,0:T(8,128)S(1)}, u32[]{:S(2)}, u32[]{:S(2)}) collective-permute-start(f32[17,8,128]{2,1,0:T(8,128)} %get-tuple-element.33), channel_id=1, source_target_pairs={{0,12},{4,0},{8,4},{12,8},{1,13},{5,1},{9,5},{13,9},{2,14},{6,2},{... | collective-permute-start | bytes 208904 | tf_op jit(solution)/shard_map/ppermute | solution.py:331
  20.2 7.6 %all-to-all-done.refs_0_ = f32[4,34,8,128]{3,2,1,0:T(8,128)S(1)} async-done(((f32[4,34,8,128]{3,2,1,0:T(8,128)}), f32[4,34,8,128]{3,2,1,0:T(8,128)S(1)}, u32[]{:S(2)}, u32[]{:S(2)}) %all-to-all-start) | async-done | bytes 557088 | tf_op jit(solution)/shard_map/all_to_all | solution.py:332
  28.0 1.9 %collective-permute-start = (f32[2,5,4,8,128]{4,3,2,1,0:T(8,128)S(1)}, f32[2,5,4,8,128]{4,3,2,1,0:T(8,128)S(1)}, u32[]{:S(2)}, u32[]{:S(2)}) collective-permute-start(f32[2,5,4,8,128]{4,3,2,1,0:T(8,128)S(1)} %get-tuple-element.23.end_other), channel_id=1, source_target_pairs={{0,16},{16,0},{32,48},{48,32},{64,80},{80,64},{96,112},{112,96},{1... | collective-permute-start | bytes 491528 | tf_op jit(solution)/shard_map/ppermute | solution.py:343
  30.0 0.9 copy-done
  31.1 3.2 %collective-permute-start.5 = (f32[34,8,128]{2,1,0:T(8,128)S(1)}, f32[34,8,128]{2,1,0:T(8,128)S(1)}, u32[]{:S(2)}, u32[]{:S(2)}) collective-permute-start(f32[34,8,128]{2,1,0:T(8,128)S(1)} %get-tuple-element.34), channel_id=1, source_target_pairs={{16,32},{32,16},{48,64},{64,48},{80,96},{96,80},{112,128},{128,112... | collective-permute-start | bytes 417800 | tf_op jit(solution)/shard_map/ppermute | solution.py:338
  34.4 1.1 %shard_map.88.table = f32[2,8,2,5,4,8,128]{6,5,4,3,2,1,0:T(8,128)S(1)} custom-call(f32[2,5,4,8,128]{4,3,2,1,0:T(8,128)S(1)} %get-tuple-element.26.cells, f32[2,2,8,128]{3,2,1,0:T(8,128)S(1)} %shard_map.87.coeffs), custom_call_target="tpu_custom_call" | custom-call | tf_op jit(solution)/shard_map/pallas_call | solution.py:32
  35.5 1.4 %shard_map.89 = (f32[2,5,4,8,128]{4,3,2,1,0:T(8,128)S(1)}, f32[2,5,4,8,128]{4,3,2,1,0:T(8,128)S(1)}, f32[34,8,128]{2,1,0:T(8,128)S(1)}) custom-call(f32[2,5,4,8,128]{4,3,2,1,0:T(8,128)S(1)} %collective-permute-done.entry, f32[2,5,4,8,128]{4,3,2,1,0:T(8,128)S(1)} %get-tuple-element.24.start_other, f32[2,5,4,8,128]{4,3,2,1,0:T(8,128)S(1)} %get-tuple-element.23.end_other, ...), custom_call_target="tpu_custom_call" | custom-call | tf_op jit(solution)/shard_map/pallas_call | solution.py:32
  36.9 6.6 %collective-permute-done.5.entry = f32[34,8,128]{2,1,0:T(8,128)S(1)} collective-permute-done((f32[34,8,128]{2,1,0:T(8,128)S(1)}, f32[34,8,128]{2,1,0:T(8,128)S(1)}, u32[]{:S(2)}, u32[]{:S(2)}) %collective-permute-start.5) | collective-permute-done | bytes 139296 | tf_op jit(solution)/shard_map/ppermute | solution.py:338
  43.6 1.4 %shard_map.91 = (f32[2,5,4,8,128]{4,3,2,1,0:T(8,128)S(1)}, f32[2,5,4,8,128]{4,3,2,1,0:T(8,128)S(1)}) custom-call(f32[34,8,128]{2,1,0:T(8,128)S(1)} %collective-permute-done.5.entry, f32[2,5,4,8,128]{4,3,2,1,0:T(8,128)S(1)} %get-tuple-element.35.start_other, f32[2,5,4,8,128]{4,3,2,1,0:T(8,128)S(1)} %get-tuple-element.36.end_other, ...), custom_call_target="tpu_custom_call" | custom-call | tf_op jit(solution)/shard_map/pallas_call | solution.py:32
  45.0 1.9 %collective-permute-start.6 = (f32[2,5,4,8,128]{4,3,2,1,0:T(8,128)S(1)}, f32[2,5,4,8,128]{4,3,2,1,0:T(8,128)S(1)}, u32[]{:S(2)}, u32[]{:S(2)}) collective-permute-start(f32[2,5,4,8,128]{4,3,2,1,0:T(8,128)S(1)} %get-tuple-element.37.end_other), channel_id=1, source_target_pairs={{0,16},{16,0},{32,48},{48,32},{64,80},{80,64},{96,112},{112,96},{1... | collective-permute-start | bytes 491528 | tf_op jit(solution)/shard_map/ppermute | solution.py:361
  46.9 6.2 %collective-permute-start.1 = (f32[34,8,128]{2,1,0:T(8,128)S(1)}, f32[34,8,128]{2,1,0:T(8,128)S(1)}, u32[]{:S(2)}, u32[]{:S(2)}) collective-permute-start(f32[34,8,128]{2,1,0:T(8,128)S(1)} %get-tuple-element.27), channel_id=1, source_target_pairs={{16,32},{32,16},{48,64},{64,48},{80,96},{96,80},{112,128},{128,112... | collective-permute-start | bytes 417800 | tf_op jit(solution)/shard_map/ppermute | solution.py:359
  53.1 1.4 %shard_map.92.refs_0_ = f32[4,2,2,4,8,128]{5,4,3,2,1,0:T(8,128)S(1)} custom-call(f32[2,5,4,8,128]{4,3,2,1,0:T(8,128)S(1)} %collective-permute-done.6.entry, f32[2,5,4,8,128]{4,3,2,1,0:T(8,128)S(1)} %get-tuple-element.38.start_other, f32[2,5,4,8,128]{4,3,2,1,0:T(8,128)S(1)} %get-tuple-element.37.end_other, ...), custom_call_target="tpu_custom_call" | custom-call | tf_op jit(solution)/shard_map/pallas_call | solution.py:32
  54.5 4.9 %collective-permute-done.1.entry = f32[34,8,128]{2,1,0:T(8,128)S(1)} collective-permute-done((f32[34,8,128]{2,1,0:T(8,128)S(1)}, f32[34,8,128]{2,1,0:T(8,128)S(1)}, u32[]{:S(2)}, u32[]{:S(2)}) %collective-permute-start.1) | collective-permute-done | bytes 139296 | tf_op jit(solution)/shard_map/ppermute | solution.py:359
  59.4 1.5 %shard_map.93 = f32[4,4,2,4,8,128]{5,4,3,2,1,0:T(8,128)S(1)} custom-call(f32[34,8,128]{2,1,0:T(8,128)S(1)} %collective-permute-done.1.entry, f32[2,5,4,8,128]{4,3,2,1,0:T(8,128)S(1)} %get-tuple-element.28.refs_0_.start_other, f32[2,5,4,8,128]{4,3,2,1,0:T(8,128)S(1)} %get-tuple-element.29.end_other, f32[2,5,4,8,128]{4,3,2,1,0:T(8,128)S(1)} %get-tuple-element.25.coupling, ...), custom_call_target="tpu_custom_call" | custom-call | tf_op jit(solution)/shard_map/pallas_call | solution.py:32
  60.9 17.6 %all_to_all.15.recv = f32[4,4,2,4,8,128]{5,4,3,2,1,0:T(8,128)S(1)} all-to-all(f32[4,4,2,4,8,128]{5,4,3,2,1,0:T(8,128)S(1)} %shard_map.93), channel_id=1, replica_groups=mesh['depth'=32,'strip'=4,'freq'=4] {'strip'}, dimensions={0} | all-to-all | bytes 1048576 | tf_op jit(solution)/shard_map/all_to_all | solution.py:364
  78.5 0.7 shard_map.95
  79.2 4.3 %all-to-all-start.2 = ((f32[4,2,2,2,8,128]{5,4,3,2,1,0:T(8,128)}), f32[4,2,2,2,8,128]{5,4,3,2,1,0:T(8,128)S(1)}, u32[]{:S(2)}, u32[]{:S(2)}) async-start(f32[4,2,2,2,8,128]{5,4,3,2,1,0:T(8,128)} %shard_map.95), calls=%async_computation.2 | async-start | bytes 262144 | tf_op jit(solution)/shard_map/all_to_all | solution.py:366
  83.5 0.8 shard_map.94
  84.3 5.2 %all-to-all-done.2.recv = f32[4,2,2,2,8,128]{5,4,3,2,1,0:T(8,128)S(1)} async-done(((f32[4,2,2,2,8,128]{5,4,3,2,1,0:T(8,128)}), f32[4,2,2,2,8,128]{5,4,3,2,1,0:T(8,128)S(1)}, u32[]{:S(2)}, u32[]{:S(2)}) %all-to-all-start.2) | async-done | bytes 131104 | tf_op jit(solution)/shard_map/all_to_all | solution.py:366
  89.5 0.6 shard_map.96
  (13 shorter events, 0.5 us)
Async XLA Ops:
  0.6 33.7 %copy-start.1 = (f32[64,2,2,8]{0,3,2,1:T(8,128)S(1)}, f32[64,2,2,8]{0,3,2,1:T(8,128)}, u32[]{:S(2)}) copy-start(f32[64,2,2,8]{0,3,2,1:T(8,128)} %param.11) | copy-start | bytes 24580
  2.7 25.1 %all-to-all-start = ((f32[4,34,8,128]{3,2,1,0:T(8,128)}), f32[4,34,8,128]{3,2,1,0:T(8,128)S(1)}, u32[]{:S(2)}, u32[]{:S(2)}) async-start(f32[4,34,8,128]{3,2,1,0:T(8,128)} %get-tuple-element.22), calls=%async_computation | async-start | bytes 1114112 | tf_op jit(solution)/shard_map/all_to_all | solution.py:332
  8.6 21.3 %collective-permute-start.2 = (f32[17,8,128]{2,1,0:T(8,128)}, f32[17,8,128]{2,1,0:T(8,128)S(1)}, u32[]{:S(2)}, u32[]{:S(2)}) collective-permute-start(f32[17,8,128]{2,1,0:T(8,128)} %get-tuple-element.31), channel_id=1, source_target_pairs={{0,4},{4,8},{8,12},{12,0},{1,5},{5,9},{9,13},{13,1},{2,6},{6,10},{... | collective-permute-start | bytes 208904 | tf_op jit(solution)/shard_map/ppermute | solution.py:331
  12.6 17.4 %collective-permute-start.3 = (f32[17,8,128]{2,1,0:T(8,128)}, f32[17,8,128]{2,1,0:T(8,128)S(1)}, u32[]{:S(2)}, u32[]{:S(2)}) collective-permute-start(f32[17,8,128]{2,1,0:T(8,128)} %get-tuple-element.32), channel_id=1, source_target_pairs={{0,8},{4,12},{8,0},{12,4},{1,9},{5,13},{9,1},{13,5},{2,10},{6,14},... | collective-permute-start | bytes 208904 | tf_op jit(solution)/shard_map/ppermute | solution.py:331
  16.9 13.1 %collective-permute-start.4 = (f32[17,8,128]{2,1,0:T(8,128)}, f32[17,8,128]{2,1,0:T(8,128)S(1)}, u32[]{:S(2)}, u32[]{:S(2)}) collective-permute-start(f32[17,8,128]{2,1,0:T(8,128)} %get-tuple-element.33), channel_id=1, source_target_pairs={{0,12},{4,0},{8,4},{12,8},{1,13},{5,1},{9,5},{13,9},{2,14},{6,2},{... | collective-permute-start | bytes 208904 | tf_op jit(solution)/shard_map/ppermute | solution.py:331
  28.0 7.5 %collective-permute-start = (f32[2,5,4,8,128]{4,3,2,1,0:T(8,128)S(1)}, f32[2,5,4,8,128]{4,3,2,1,0:T(8,128)S(1)}, u32[]{:S(2)}, u32[]{:S(2)}) collective-permute-start(f32[2,5,4,8,128]{4,3,2,1,0:T(8,128)S(1)} %get-tuple-element.23.end_other), channel_id=1, source_target_pairs={{0,16},{16,0},{32,48},{48,32},{64,80},{80,64},{96,112},{112,96},{1... | collective-permute-start | bytes 491528 | tf_op jit(solution)/shard_map/ppermute | solution.py:343
  30.0 0.9 copy-start
  31.1 12.5 %collective-permute-start.5 = (f32[34,8,128]{2,1,0:T(8,128)S(1)}, f32[34,8,128]{2,1,0:T(8,128)S(1)}, u32[]{:S(2)}, u32[]{:S(2)}) collective-permute-start(f32[34,8,128]{2,1,0:T(8,128)S(1)} %get-tuple-element.34), channel_id=1, source_target_pairs={{16,32},{32,16},{48,64},{64,48},{80,96},{96,80},{112,128},{128,112... | collective-permute-start | bytes 417800 | tf_op jit(solution)/shard_map/ppermute | solution.py:338
  45.0 8.1 %collective-permute-start.6 = (f32[2,5,4,8,128]{4,3,2,1,0:T(8,128)S(1)}, f32[2,5,4,8,128]{4,3,2,1,0:T(8,128)S(1)}, u32[]{:S(2)}, u32[]{:S(2)}) collective-permute-start(f32[2,5,4,8,128]{4,3,2,1,0:T(8,128)S(1)} %get-tuple-element.37.end_other), channel_id=1, source_target_pairs={{0,16},{16,0},{32,48},{48,32},{64,80},{80,64},{96,112},{112,96},{1... | collective-permute-start | bytes 491528 | tf_op jit(solution)/shard_map/ppermute | solution.py:361
  46.9 12.5 %collective-permute-start.1 = (f32[34,8,128]{2,1,0:T(8,128)S(1)}, f32[34,8,128]{2,1,0:T(8,128)S(1)}, u32[]{:S(2)}, u32[]{:S(2)}) collective-permute-start(f32[34,8,128]{2,1,0:T(8,128)S(1)} %get-tuple-element.27), channel_id=1, source_target_pairs={{16,32},{32,16},{48,64},{64,48},{80,96},{96,80},{112,128},{128,112... | collective-permute-start | bytes 417800 | tf_op jit(solution)/shard_map/ppermute | solution.py:359
  79.2 10.3 %all-to-all-start.2 = ((f32[4,2,2,2,8,128]{5,4,3,2,1,0:T(8,128)}), f32[4,2,2,2,8,128]{5,4,3,2,1,0:T(8,128)S(1)}, u32[]{:S(2)}, u32[]{:S(2)}) async-start(f32[4,2,2,2,8,128]{5,4,3,2,1,0:T(8,128)} %shard_map.95), calls=%async_computation.2 | async-start | bytes 262144 | tf_op jit(solution)/shard_map/all_to_all | solution.py:366
